TPU v7x, 128 devices: a whole 4x4x4 slice. The times are simulated.
128 devices in a mesh: seq: 8 (over x, core), tensor: 16 (over y, z).
Axes of the slice: x: 4, y: 4, z: 4, core: 2. Of those that a mesh axis runs over, the one named last changes fastest.
Arguments:
- hidden_in: bfloat16 [8192, 2048], P('seq'), may hold values from -6 to 6
- gain_attn: float32 [2048], replicated, may hold values from 0.1 to 1.9
- gain_mlp: float32 [2048], replicated, may hold values from 0.1 to 1.9
- w_qkv: bfloat16 [3, 2048, 2048], P(None, None, 'tensor')
- w_attn_out: bfloat16 [2048, 2048], P('tensor'), may hold values from -0.125 to 0.125
- w_mlp_in: bfloat16 [2048, 8192], P(None, 'tensor'), may hold values from -0.125 to 0.125
- w_mlp_out: bfloat16 [8192, 2048], P('tensor'), may hold values from -0.0625 to 0.0625
- segment_ids: int32 [8192], P('seq'), may hold values from 0 to 1, as said below
- positions: int32 [8192], P('seq'), may hold values from 0 to 8191, as said below
- kv_prefill: bfloat16 [128, 8, 2, 64, 2048], P('seq', None, None, None, 'tensor'), may hold values from -6 to 6
- page_source: int32 [128], replicated, may hold values from 0 to 127, as said below
Outputs:
- hidden_out: bfloat16 [8192, 2048], P('seq')
- kv_decode: bfloat16 [128, 8, 2, 64, 2048], P('tensor', None, None, None, 'seq')
Inputs may be any that keep to these rules, and one draw needn't show every extreme that they name: `segment_ids`: never falling along the span; two prompts, each a multiple of 64 tokens long, the first of 2048 to 6144 tokens. `positions`: within a prompt, consecutive from the prompt's first position; the second prompt starts at 0 and the first at the second prompt's length. `page_source`: a permutation; page g * 8 + r + j (j below 1, r below 8) takes a block of the r-th aligned run of 16 blocks.
All inputs are finite; a program needn't handle non-finite values.
Results may differ from a plain program's by a relative error of at most 0.015.
The roundings to bfloat16 on the way count: a program that leaves them out, or rounds other values in their place, can miss the bound.
Values may be sent and summed in bfloat16 or wider, within the bound.
A program may use at most 128 MiB of HBM per device.

v0:
```python
import jax
import jax.numpy as jnp
from jax import lax
from jax.sharding import PartitionSpec as P

HEADS = 8
HD = 256


def partner(block, axis, bit):
    count = lax.axis_size(axis)
    route = []
    for low in range(count):
        high = low | 1 << bit
        if high != low and high < count:
            route += [(low, high), (high, low)]
    return lax.ppermute(block, axis, route)


def layer_norm(values, gain_vec):
    mean_val = jnp.mean(values, axis=-1, keepdims=True)
    centered = values - mean_val
    spread_sq = jnp.mean(centered * centered, axis=-1, keepdims=True)
    return centered * lax.rsqrt(spread_sq + 1e-05) * gain_vec


def rotate(values, positions):
    rot_dims = HD // 4
    half_dims = rot_dims // 2
    freqs = 10000.0 ** (-(jnp.arange(half_dims, dtype=jnp.float32) * 2.0 / rot_dims))
    angles = positions.astype(jnp.float32)[:, None] * freqs[None, :]
    cosine = jnp.cos(angles)
    sine = jnp.sin(angles)
    first_half = values[:, :half_dims]
    second_half = values[:, half_dims:rot_dims]
    return jnp.concatenate(
        [
            first_half * cosine - second_half * sine,
            second_half * cosine + first_half * sine,
            values[:, rot_dims:],
        ],
        axis=1,
    )


def on_device(
    hidden_in,
    gain_attn,
    gain_mlp,
    w_qkv,
    w_attn_out,
    w_mlp_in,
    w_mlp_out,
    segment_ids,
    positions,
    kv_prefill,
    page_source,
):
    seq_row = lax.axis_index("seq")
    seq_count = lax.axis_size("seq")
    n_tensor = lax.axis_size("tensor")
    block_rows = kv_prefill.shape[0]
    group_blocks = block_rows // n_tensor
    group_pages = group_blocks * seq_count
    page_slots = (
        jnp.arange(n_tensor, dtype=jnp.int32)[:, None] * group_pages
        + seq_row * group_blocks
        + jnp.arange(group_blocks, dtype=jnp.int32)[None, :]
    ).reshape(block_rows)
    local_order = jnp.take(page_source, page_slots) - seq_row * block_rows
    ordered = jnp.take(kv_prefill, local_order, axis=0)
    kv_decode = lax.all_to_all(
        lax.all_to_all(ordered, "tensor", split_axis=0, concat_axis=4, tiled=True),
        "seq",
        split_axis=4,
        concat_axis=0,
        tiled=True,
    )
    tok_rows = hidden_in.shape[0]
    group_size = n_tensor // HEADS
    head_part = lax.axis_index("tensor") % group_size
    values = hidden_in.astype(jnp.float32)
    normed_attn = layer_norm(values, gain_attn).astype(jnp.bfloat16)
    normed_mlp = layer_norm(values, gain_mlp).astype(jnp.bfloat16)
    projected = jnp.einsum("td,kdc->ktc", normed_attn, w_qkv, preferred_element_type=jnp.float32)
    turned = jnp.stack(
        [rotate(projected[0], positions), rotate(projected[1], positions), projected[2]]
    )
    projected = jnp.where(head_part == 0, turned, projected).astype(jnp.bfloat16)
    other_qkv, other_out = partner((projected, w_attn_out), "tensor", 0)
    is_lower = head_part == 0
    heads_qkv = jnp.concatenate(
        [jnp.where(is_lower, projected, other_qkv), jnp.where(is_lower, other_qkv, projected)],
        axis=2,
    )
    heads_out = jnp.concatenate(
        [jnp.where(is_lower, w_attn_out, other_out), jnp.where(is_lower, other_out, w_attn_out)],
        axis=0,
    )
    piece_rows = tok_rows // (2 * group_size)
    row_starts = (2 * head_part * piece_rows, (2 * head_part + 1) * piece_rows)
    queries = jnp.concatenate(
        [
            lax.dynamic_slice_in_dim(heads_qkv[0], first_row, piece_rows, 0)
            for first_row in row_starts
        ],
        axis=0,
    )
    local_ids = jnp.concatenate(
        [first_row + jnp.arange(piece_rows, dtype=jnp.int32) for first_row in row_starts]
    )
    query_ids = seq_row * tok_rows + local_ids
    query_segs = jnp.take(segment_ids, local_ids)
    query_last = jnp.max(query_ids)
    seg_first = jnp.min(query_segs)
    scale = heads_qkv.shape[2] ** (-0.5)

    def update(state_now, key_block, val_block, seg_block, block_start):
        run_max, run_sum, run_acc = state_now
        scores = (
            jnp.einsum("qc,kc->qk", queries, key_block, preferred_element_type=jnp.float32) * scale
        )
        key_ids = block_start + jnp.arange(key_block.shape[0], dtype=jnp.int32)
        allowed = (seg_block[None, :] == query_segs[:, None]) & (
            key_ids[None, :] <= query_ids[:, None]
        )
        scores = jnp.where(allowed, scores, -1e30)
        new_max = jnp.maximum(run_max, jnp.max(scores, axis=1))
        keep_factor = jnp.exp(run_max - new_max)
        weights = jnp.where(allowed, jnp.exp(scores - new_max[:, None]), 0.0)
        new_sum = run_sum * keep_factor + jnp.sum(weights, axis=1)
        new_acc = run_acc * keep_factor[:, None] + jnp.dot(
            weights.astype(jnp.bfloat16), val_block, preferred_element_type=jnp.float32
        )
        return (new_max, new_sum, new_acc)

    query_count = queries.shape[0]
    head_dims = heads_qkv.shape[2]
    start_state = (
        jnp.full((query_count,), -1e30, jnp.float32),
        jnp.zeros((query_count,), jnp.float32),
        jnp.zeros((query_count, head_dims), jnp.float32),
    )
    key_rows = lax.all_gather(heads_qkv[1], "seq", axis=0, tiled=True)
    val_rows = lax.all_gather(heads_qkv[2], "seq", axis=0, tiled=True)
    seg_rows = lax.all_gather(segment_ids, "seq", axis=0, tiled=True)
    shard_count = key_rows.shape[0] // tok_rows
    blocks = (
        key_rows.reshape(shard_count, tok_rows, key_rows.shape[1]),
        val_rows.reshape(shard_count, tok_rows, val_rows.shape[1]),
        seg_rows.reshape(shard_count, tok_rows),
        tok_rows * jnp.arange(shard_count, dtype=jnp.int32),
    )

    def one_block(state_in, block):
        key_block, val_block, seg_block, block_start = block
        active = (block_start <= query_last) & (seg_block[tok_rows - 1] >= seg_first)
        state_out = lax.cond(
            active,
            lambda state_arg: update(state_arg, key_block, val_block, seg_block, block_start),
            lambda state_arg: state_arg,
            state_in,
        )
        return (state_out, None)

    state_end, unused = lax.scan(one_block, start_state, blocks)
    run_max, run_sum, run_acc = state_end
    attended = (run_acc / run_sum[:, None]).astype(jnp.bfloat16)
    attn_rows = jnp.dot(attended, heads_out, preferred_element_type=jnp.float32)
    attn_full = jnp.zeros((tok_rows, attn_rows.shape[1]), jnp.float32)
    attn_full = lax.dynamic_update_slice_in_dim(attn_full, attn_rows[:piece_rows], row_starts[0], 0)
    attn_full = lax.dynamic_update_slice_in_dim(attn_full, attn_rows[piece_rows:], row_starts[1], 0)
    hidden_mlp = jax.nn.gelu(
        jnp.dot(normed_mlp, w_mlp_in, preferred_element_type=jnp.float32), approximate=False
    ).astype(jnp.bfloat16)
    branch_total = lax.psum(
        (attn_full + jnp.dot(hidden_mlp, w_mlp_out, preferred_element_type=jnp.float32)).astype(
            jnp.bfloat16
        ),
        "tensor",
    ).astype(jnp.float32)
    hidden_out = (values + branch_total).astype(jnp.bfloat16)
    return (hidden_out, kv_decode)


def solution(mesh):
    placed = (
        P("seq", None),
        P(),
        P(),
        P(None, None, "tensor"),
        P("tensor", None),
        P(None, "tensor"),
        P("tensor", None),
        P("seq"),
        P("seq"),
        P("seq", None, None, None, "tensor"),
        P(),
    )
    return jax.shard_map(
        on_device,
        mesh=mesh,
        in_specs=placed,
        out_specs=(P("seq", None), P("tensor", None, None, None, "seq")),
        check_vma=False,
    )
```

profile of v0, /device:TPU:6, one launch (start us, length us, event | category | flops | bytes accessed | tf_op | source)
XLA Modules:
  0.0 327.2 jit_solution(137620122876999214)
XLA Ops:
  7.3 3.0 convert_reduce_fusion
  12.1 2.6 copy.23
  14.7 4.7 %fusion.32 = f32[1024,384]{0,1:S(1)} fusion(bf16[2048,384]{0,1:T(8,128)(2,1)} %bitcast.78, bf16[1024,2048]{1,0:T(8,128)(2,1)} %param.15, f32[2048]{0:T(1024)S(1)} %copy-done.9, f32[1024]{0:T(1024)S(1)} %add_rsqrt_fusion, f32[1024]{0:T(1024)S(1)} %broadcast_multiply_fusion), kind=kOutput, calls=%fused_computation.45 | convolution fusion | flops 1621098496 | bytes 7356416
  22.2 2.0 collective-permute-start
  24.2 17.5 %collective-permute-done = bf16[3,1024,128]{1,2,0:T(8,128)(2,1)S(1)} collective-permute-done((bf16[3,1024,128]{1,2,0:T(8,128)(2,1)S(1)}, bf16[3,1024,128]{1,2,0:T(8,128)(2,1)S(1)}, u32[]{:S(2)}, u32[]{:S(2)}) %collective-permute-start) | collective-permute-done | bytes 786464 | tf_op jit(solution)/shard_map/ppermute | solution.py:17
  46.8 5.3 %gather_fusion.2 = bf16[16,8,2,64,128]{4,3,2,1,0:T(8,128)(2,1)} fusion(bf16[16,8,2,64,128]{4,3,2,1,0:T(8,128)(2,1)} %param.24, s32[1024]{0:T(1024)S(1)} %pad_clamp_fusion), kind=kCustom, calls=%fused_computation.2 | custom fusion | bytes 8388672 | tf_op jit(solution)/shard_map/jit(_take)/gather | solution.py:71
  52.1 4.6 %broadcast_select_fusion = bf16[16,8,2,64,128]{4,3,2,1,0:T(8,128)(2,1)} fusion(bf16[16,8,2,64,128]{4,3,2,1,0:T(8,128)(2,1)} %gather_fusion.2, pred[16]{0:T(512)(128)(4,1)S(1)} %compare_and_fusion.1), kind=kLoop, calls=%fused_computation.52 | loop fusion | flops 2097152 | bytes 8388624 | tf_op jit(solution)/shard_map/jit(_take)/select_n | solution.py:71
  56.7 7.9 %all-to-all-start = ((bf16[16,8,2,64,128]{4,3,2,1,0:T(8,128)(2,1)}), bf16[16,8,2,64,128]{4,3,2,1,0:T(8,128)(2,1)}, u32[]{:S(2)}, u32[]{:S(2)}) async-start(bf16[16,8,2,64,128]{4,3,2,1,0:T(8,128)(2,1)} %broadcast_select_fusion), calls=%async_computation | async-start | bytes 8388608 | tf_op jit(solution)/shard_map/all_to_all | solution.py:73
  64.7 2.3 gather_fusion
  67.0 13.2 %all_gather.9 = s32[8192]{0:T(1024)S(1)} all-gather(s32[1024]{0:T(1024)S(1)} %copy-done.2), channel_id=1, replica_groups=mesh['seq'=8,'tensor'=16] {'seq'}, dimensions={0}, use_global_device_ids=true | all-gather | bytes 36864 | tf_op jit(solution)/shard_map/all_gather | solution.py:146
  81.0 2.1 broadcast_select_fusion.4
  84.3 6.4 %copy.32 = bf16[1,8192,256]{2,1,0:T(8,128)(2,1)} copy(bf16[1,8192,256]{1,2,0:T(8,128)(2,1)} %all-gather.5.cloned.1.call-done) | data formatting | bytes 8388608 | tf_op jit(solution)/shard_map/while | solution.py:166
  90.7 19.6 %all-gather.7.cloned.1.call-done = bf16[1,8192,256]{1,2,0:T(8,128)(2,1)} async-done(((bf16[1,1024,256]{1,2,0:T(8,128)(2,1)}), bf16[1,8192,256]{1,2,0:T(8,128)(2,1)}) %all-gather.7.cloned.1.call-update) | async-done | bytes 4194320 | tf_op jit(solution)/shard_map/all_gather | solution.py:145
  110.3 6.4 %copy.33 = bf16[1,8192,256]{2,1,0:T(8,128)(2,1)} copy(bf16[1,8192,256]{1,2,0:T(8,128)(2,1)} %all-gather.7.cloned.1.call-done) | data formatting | bytes 8388608 | tf_op jit(solution)/shard_map/while | solution.py:166
  116.7 53.3 %while.14 = (s32[]{:T(128)}, f32[512]{0:T(512)S(1)}, f32[512]{0:T(512)S(1)}, f32[512,256]{1,0:T(8,128)S(1)}, s32[8]{0:T(128)S(1)}, /*index=5*/s32[]{:T(128)}, s3...) while((s32[]{:T(128)}, f32[512]{0:T(512)S(1)}, ...), condition=%wide.region_9.10_spmd, body=%wide.region_4.9_spmd.sunk | while | flops 548669440 | bytes 8734059 | solution.py:166
  132.1 5.7 %conditional.2 = ((f32[512]{0:T(512)S(1)}, f32[512]{0:T(512)S(1)}, f32[512,256]{1,0:T(8,128)S(1)})) conditional(s32[]{:T(128)} %convert_element_type.94, (f32[512]{0:T(512)S(1)}, f32[512]{0:T(512)S(1)}, f32[512,256]{1,0:T(8,128)S(1)}) %tuple.57, (s32[1,1024]{1,0:T(1,128)S(1)}, s32[512]{0:T(512)S(1)}, s32[]{:T(128)}, s32[512]{0:T(512)S(1)}, ...), branch_computations={%region_5.5_spmd, %region_6.8_spmd} | conditional | flops 548669440 | bytes 8725540 | solution.py:158
  135.5 2.2 convolution_add_fusion
  141.6 5.7 %conditional.2 = ((f32[512]{0:T(512)S(1)}, f32[512]{0:T(512)S(1)}, f32[512,256]{1,0:T(8,128)S(1)})) conditional(s32[]{:T(128)} %convert_element_type.94, (f32[512]{0:T(512)S(1)}, f32[512]{0:T(512)S(1)}, f32[512,256]{1,0:T(8,128)S(1)}) %tuple.57, (s32[1,1024]{1,0:T(1,128)S(1)}, s32[512]{0:T(512)S(1)}, s32[]{:T(128)}, s32[512]{0:T(512)S(1)}, ...), branch_computations={%region_5.5_spmd, %region_6.8_spmd} | conditional | flops 548669440 | bytes 8725540 | solution.py:158
  145.0 2.2 convolution_add_fusion
  151.1 5.7 %conditional.2 = ((f32[512]{0:T(512)S(1)}, f32[512]{0:T(512)S(1)}, f32[512,256]{1,0:T(8,128)S(1)})) conditional(s32[]{:T(128)} %convert_element_type.94, (f32[512]{0:T(512)S(1)}, f32[512]{0:T(512)S(1)}, f32[512,256]{1,0:T(8,128)S(1)}) %tuple.57, (s32[1,1024]{1,0:T(1,128)S(1)}, s32[512]{0:T(512)S(1)}, s32[]{:T(128)}, s32[512]{0:T(512)S(1)}, ...), branch_computations={%region_5.5_spmd, %region_6.8_spmd} | conditional | flops 548669440 | bytes 8725540 | solution.py:158
  154.5 2.2 convolution_add_fusion
  160.6 5.7 %conditional.2 = ((f32[512]{0:T(512)S(1)}, f32[512]{0:T(512)S(1)}, f32[512,256]{1,0:T(8,128)S(1)})) conditional(s32[]{:T(128)} %convert_element_type.94, (f32[512]{0:T(512)S(1)}, f32[512]{0:T(512)S(1)}, f32[512,256]{1,0:T(8,128)S(1)}) %tuple.57, (s32[1,1024]{1,0:T(1,128)S(1)}, s32[512]{0:T(512)S(1)}, s32[]{:T(128)}, s32[512]{0:T(512)S(1)}, ...), branch_computations={%region_5.5_spmd, %region_6.8_spmd} | conditional | flops 548669440 | bytes 8725540 | solution.py:158
  161.2 1.8 fusion
  164.0 2.2 convolution_add_fusion
  171.9 4.3 %broadcast_in_dim.59 = f32[1024,2048]{1,0:T(8,128)} broadcast(f32[]{:T(128)} %constant.69.clone.1), dimensions={} | broadcast | bytes 8388612 | tf_op jit(solution)/shard_map/broadcast_in_dim | solution.py:170
  179.1 14.2 %add_convert_fusion = bf16[1024,2048]{1,0:T(8,128)(2,1)} fusion(f32[1024,2048]{1,0:T(8,128)} %slice_dynamic-update-slice_fusion, bf16[512,2048]{1,0:T(8,128)(2,1)S(1)} %copy-done, bf16[2048,512]{1,0:T(8,128)(2,1)} %param.20, bf16[1024,2048]{1,0:T(8,128)(2,1)} %param.15, f32[2048]{0:T(1024)S(1)} %copy-done.10, f32[1024]{0:T(1024)S(1)} %add_rsqrt_fusion, ...), kind=kOutput, calls=%fused_computation.43 | convolution fusion | flops 4343726080 | bytes 20987904 | tf_op jit(solution)/shard_map/dot_general | solution.py:177
  193.3 20.6 %copy.34 = bf16[1,8,2,64,16,128]{3,2,1,5,4,0:T(2,128)(2,1)} copy(bf16[1,8,2,64,16,128]{5,3,2,1,4,0:T(8,128)(2,1)} %bitcast.26) | data formatting | bytes 8388608 | tf_op jit(solution)/shard_map/all_to_all | solution.py:73
  213.9 10.6 %reshape.206 = bf16[8,2,131072]{2,1,0:T(2,128)(2,1)} reshape(bf16[2048,1,8,2,64]{4,3,2,1,0:T(2,128)(2,1)} %bitcast.69) | data formatting | bytes 8388608
  224.5 57.8 %all_to_all.36 = bf16[8,2,131072]{2,1,0:T(2,128)(2,1)} all-to-all(bf16[8,2,131072]{2,1,0:T(2,128)(2,1)} %reshape.206), channel_id=1, replica_groups=mesh['seq'=8,'tensor'=16] {'seq'}, dimensions={0} | all-to-all | bytes 8388608 | tf_op jit(solution)/shard_map/all_to_all | solution.py:72
  282.3 10.4 %reshape.207 = bf16[2048,1,8,2,64]{4,3,2,1,0:T(2,128)(2,1)} reshape(bf16[8,2,131072]{2,1,0:T(2,128)(2,1)} %all_to_all.36) | data formatting | bytes 8388608
  292.7 20.0 %copy.36 = bf16[1,8,2,64,8,256]{5,3,2,1,4,0:T(8,128)(2,1)} copy(bf16[1,8,2,64,8,256]{3,2,1,5,4,0:T(2,128)(2,1)} %bitcast.70) | data formatting | bytes 8388608 | tf_op jit(solution)/shard_map/all_to_all | solution.py:72
  312.7 7.9 %fusion.29 = bf16[1024,2048]{1,0:T(8,128)(2,1)} fusion(bf16[1024,2048]{1,0:T(8,128)(2,1)} %param.15, bf16[1024,2048]{1,0:T(8,128)(2,1)} %all-reduce.2.cloned.1.call-done), kind=kLoop, calls=%fused_computation.42 | loop fusion | flops 8388608 | bytes 12582912 | tf_op jit(solution)/shard_map/convert_element_type | solution.py:182
  (121 shorter events, 38.5 us)
Async XLA Ops:
  7.2 172.0 %copy-start = (bf16[512,2048]{1,0:T(8,128)(2,1)S(1)}, bf16[512,2048]{1,0:T(8,128)(2,1)}, u32[]{:S(2)}) copy-start(bf16[512,2048]{1,0:T(8,128)(2,1)} %param.21) | copy-start | bytes 6291460
  7.2 77.1 %all-gather.5.cloned.1.call-start = ((), (), s32[]{:S(2)}) async-start(), calls=%async_computation.3 | async-start | bytes 4718592 | tf_op jit(solution)/shard_map/all_gather | solution.py:144
  7.2 3.6 %copy-start.4 = (bf16[1024,2048]{1,0:T(8,128)(2,1)S(1)}, bf16[1024,2048]{1,0:T(8,128)(2,1)}, u32[]{:S(2)}) copy-start(bf16[1024,2048]{1,0:T(8,128)(2,1)} %param.15) | copy-start | bytes 12582916
  12.1 2.6 copy-start.9
  19.3 1.1 copy-start.5
  19.4 1.2 copy-start.8
  20.6 1.4 copy-start.6
  22.2 19.5 %collective-permute-start = (bf16[3,1024,128]{1,2,0:T(8,128)(2,1)S(1)}, bf16[3,1024,128]{1,2,0:T(8,128)(2,1)S(1)}, u32[]{:S(2)}, u32[]{:S(2)}) collective-permute-start(bf16[3,1024,128]{1,2,0:T(8,128)(2,1)S(1)} %fusion.50), channel_id=1, source_target_pairs={{0,1},{1,0},{2,3},{3,2},{4,5},{5,4},{6,7},{7,6},{8,9},{9,8},{10,11... | collective-permute-start | bytes 2359304 | tf_op jit(solution)/shard_map/ppermute | solution.py:17
  42.3 2.0 copy-start.7
  42.3 3.8 %copy-start.3 = (s32[128]{0:T(128)S(1)}, s32[128]{0:T(128)}, u32[]{:S(2)}) copy-start(s32[128]{0:T(128)} %param.25) | copy-start | bytes 1540
  43.5 66.8 %all-gather.7.cloned.1.call-start = ((), (), s32[]{:S(2)}) async-start(), calls=%async_computation.4 | async-start | bytes 4718592 | tf_op jit(solution)/shard_map/all_gather | solution.py:145
  44.3 36.7 %collective-permute-start.1 = (bf16[128,2048]{1,0:T(8,128)(2,1)S(1)}, bf16[128,2048]{1,0:T(8,128)(2,1)}, u32[]{:S(2)}, u32[]{:S(2)}) collective-permute-start(bf16[128,2048]{1,0:T(8,128)(2,1)S(1)} %copy-done.7), channel_id=1, source_target_pairs={{0,1},{1,0},{2,3},{3,2},{4,5},{5,4},{6,7},{7,6},{8,9},{9,8},{10,11... | collective-permute-start | bytes 1572872 | tf_op jit(solution)/shard_map/ppermute | solution.py:17
  56.7 8.0 %copy-start.2 = (s32[1024]{0:T(1024)S(1)}, s32[1024]{0:T(1024)}, u32[]{:S(2)}) copy-start(s32[1024]{0:T(1024)} %param.22) | copy-start | bytes 12292
  56.7 136.6 %all-to-all-start = ((bf16[16,8,2,64,128]{4,3,2,1,0:T(8,128)(2,1)}), bf16[16,8,2,64,128]{4,3,2,1,0:T(8,128)(2,1)}, u32[]{:S(2)}, u32[]{:S(2)}) async-start(bf16[16,8,2,64,128]{4,3,2,1,0:T(8,128)(2,1)} %broadcast_select_fusion), calls=%async_computation | async-start | bytes 8388608 | tf_op jit(solution)/shard_map/all_to_all | solution.py:73
  64.6 248.1 %all-reduce.2.cloned.1.call-start = ((), (), s32[]{:S(2)}) async-start(), calls=%async_computation.2 | async-start | bytes 8388608 | tf_op jit(solution)/shard_map/psum | solution.py:176
  177.7 1.5 copy-start.10
  312.7 7.9 %copy-start.1 = (bf16[512,2048]{1,0:T(8,128)(2,1)S(1)}, bf16[512,2048]{1,0:T(8,128)(2,1)}, u32[]{:S(2)}) copy-start(bf16[512,2048]{1,0:T(8,128)(2,1)} %param.21) | copy-start | bytes 6291460
Sparse Core Ops, SparseCore 0:
  43.6 32.3 all-gather.4
  78.3 31.9 all-gather.6
  193.4 110.3 all-reduce.1
where the time goes:
time: 332 us; the launch traced here: 327 us
  local copies, waits for them, and re-layouts  106 us (32%)
  blocking collectives  71 us (21%)
  waiting for transfers between devices  37.9 us (11%)
  matrix products  36.8 us (11%)
  other arithmetic  28.5 us (9%)
  loops' own time  20.7 us (6%)
  between operations  14.1 us (4%)
  starting transfers between devices  11.8 us (4%)
    all_to_all x1, blocking collectives, on_device(): lax.all_to_all(lax.all_to_all(ordered, 'tensor', split_axis=0, concat_axi...  57.8 us
    unnamed x25, local copies, waits for them, and re-layouts  26 us
    all_to_all x1, local copies, waits for them, and re-layouts, on_device(): lax.all_to_all(ordered, 'tensor', split_axis=0, concat_axis=4, tiled=True)  20.6 us
    another operation x1, loops' own time, on_device(): state_end, unused = lax.scan(one_block, start_state, blocks)  20.4 us
    all_to_all x1, local copies, waits for them, and re-layouts, on_device(): lax.all_to_all(lax.all_to_all(ordered, 'tensor', split_axis=0, concat_axi...  20 us
    all_gather x1, waiting for transfers between devices, on_device(): val_rows = lax.all_gather(heads_qkv[2], 'seq', axis=0, tiled=True)  19.6 us
    ppermute x2, waiting for transfers between devices, partner(): return lax.ppermute(block, axis, route)  17.5 us
    dot_general x1, matrix products, on_device(): jnp.dot(hidden_mlp, w_mlp_out, preferred_element_type=jnp.float32)  14.2 us
  transfers between devices with their start and end apart: 6, of which 2 were waited for; matrix products, arithmetic and copies ran while one was open for 45% of the time, Pallas kernels for 0%

commit v1 on v0

v1 whole, which is shorter than its diff:
```python
import jax
import jax.numpy as jnp
from jax import lax
from jax.experimental import pallas as pl
from jax.experimental.pallas import tpu as pltpu
from jax.sharding import PartitionSpec as P

MESH = pl.DeviceIdType.MESH
F32 = jnp.float32
BF16 = jnp.bfloat16
HD = 256
LOW = -1e30
MASKED = -3e30
TT = (((1,), (1,)), ((), ()))
FF = (((0,), (0,)), ((), ()))


def layer_kernel(
    x_hbm,
    ga_ref,
    gm_ref,
    wqkv_hbm,
    wo_hbm,
    wi_hbm,
    w2_hbm,
    cos_ref,
    sin_ref,
    first_ref,
    psrc_ref,
    kv_hbm,
    out_hbm,
    kvout_hbm,
    x_v,
    na_v,
    nm_v,
    wcat_v,
    wi_v,
    w2_v,
    wo_v,
    hid_v,
    part_v,
    kvin_v,
    kvs_v,
    bufa_v,
    bufb_v,
    kvx_v,
    kvbuf_v,
    stage_v,
    qstage_v,
    q_v,
    acc_v,
    stat_v,
    mine_v,
    theirs_v,
    direct_v,
    relay_v,
    sums_v,
    merged_v,
    fold_v,
    direct2_v,
    relay2_v,
    sums2_v,
    merged2_v,
    lsem,
    ssem,
    rsem,
    kvs_sem,
    kvr_sem,
):
    seq = lax.axis_index("seq")
    ten = lax.axis_index("tensor")
    xx = seq // 2
    core = lax.rem(seq, 2)
    yy = ten // 4
    zz = lax.rem(ten, 4)
    half = lax.rem(ten, 2)
    zh = zz // 2

    def around(value, step):
        return lax.rem(value + step + 4, 4)

    def dev(x_=None, c_=None, y_=None, z_=None):
        x_ = xx if x_ is None else x_
        c_ = core if c_ is None else c_
        y_ = yy if y_ is None else y_
        z_ = zz if z_ is None else z_
        return (x_ * 2 + c_, y_ * 4 + z_)

    counter = [0]
    pending = []

    def remote(src, dst, device):
        index = counter[0]
        counter[0] += 1
        copy = pltpu.make_async_remote_copy(
            src_ref=src,
            dst_ref=dst,
            send_sem=ssem.at[index],
            recv_sem=rsem.at[index],
            device_id=device,
            device_id_type=MESH,
        )
        pending.append(copy)
        return copy

    local_count = [0]

    def local(src, dst):
        index = local_count[0]
        local_count[0] += 1
        copy = pltpu.make_async_copy(src, dst, lsem.at[index])
        copy.start()
        return copy

    load_x = local(x_hbm, x_v)
    load_w = [local(wqkv_hbm.at[c], wcat_v.at[:, pl.ds(j * 128, 128)]) for j, c in ((0, 1), (1, 2), (2, 0))]
    load_kv = local(kv_hbm, kvin_v)
    load_wi = local(wi_hbm, wi_v)
    load_w2 = local(w2_hbm, w2_v)
    own_rows = pl.ds(pl.multiple_of(half * 128, 128), 128)
    load_wo = local(wo_hbm, wo_v.at[own_rows, :])

    barrier = pltpu.get_barrier_semaphore()
    peers = [dev(y_=around(yy, k)) for k in (1, 2, 3)]
    peers += [dev(z_=around(zz, k)) for k in (1, 2, 3)]
    peers += [(lax.rem(seq + k, 8), ten) for k in range(1, 8)]
    for peer in peers:
        pl.semaphore_signal(barrier, inc=1, device_id=peer, device_id_type=MESH)
    pl.semaphore_wait(barrier, len(peers))

    partner = dev(z_=zz + 1 - 2 * half)
    twin = (seq + 1 - 2 * core, ten)

    half_rows = pl.ds(pl.multiple_of(half * 128 + core * 64, 64), 64)
    wo_cross = remote(wo_hbm.at[pl.ds(pl.multiple_of(core * 64, 64), 64)], wo_v.at[half_rows, :], partner)
    wo_cross.start()

    load_kv.wait()

    @pl.loop(0, 16)
    def _(group):
        kvs_v[group] = kvin_v[lax.rem(psrc_ref[group * 8 + seq], 16)]

    low = pl.ds(0, 512)
    high = pl.ds(512, 512)
    col_half = pl.ds(pl.multiple_of(half * 128, 128), 128)
    a_one = []
    for k in (1, 2, 3):
        to_y = around(yy, k)
        a_one.append(remote(kvs_v.at[pl.ds(to_y * 4, 4), low], bufa_v.at[yy], dev(y_=to_y)))
        a_one[-1].start()
    a_own = local(kvs_v.at[pl.ds(yy * 4, 4), low], bufa_v.at[yy])

    load_x.wait()
    for copy in load_w:
        copy.wait()
    ga = ga_ref[...]
    gm = gm_ref[...]

    @pl.loop(0, 4)
    def _(step):
        start = lax.rem(step * 256 + (1 - half) * 512, 1024)
        rows = pl.ds(pl.multiple_of(start, 256), 256)
        values = x_v[rows, :].astype(F32)
        mean = jnp.mean(values, axis=-1, keepdims=True)
        centered = values - mean
        spread = jnp.mean(centered * centered, axis=-1, keepdims=True)
        normed = centered * lax.rsqrt(spread + 1e-05)
        na = (normed * ga).astype(BF16)
        na_v[rows, :] = na
        nm_v[rows, :] = (normed * gm).astype(BF16)
        kv = jnp.dot(na, wcat_v[:, 0:256], preferred_element_type=F32)
        q = jnp.dot(na, wcat_v[:, 256:384], preferred_element_type=F32)
        lanes = lax.broadcasted_iota(jnp.int32, (256, 128), 1)
        cosine = cos_ref[rows, :]
        sine = sin_ref[rows, :]

        def turned(values_in):
            other = jnp.where(lanes < 32, pltpu.roll(values_in, 96, 1), pltpu.roll(values_in, 32, 1))
            return values_in * cosine + other * sine

        stage_v[0, rows, :] = turned(kv[:, 0:128]).astype(BF16)
        stage_v[1, rows, :] = kv[:, 128:256].astype(BF16)
        qstage_v[rows, :] = (turned(q) * (HD**-0.5)).astype(BF16)

    own_keys = pl.ds(pl.multiple_of(half * 512, 512), 512)
    cross_keys = pl.ds(pl.multiple_of((1 - half) * 512, 512), 512)
    kv_cross = remote(stage_v.at[:, cross_keys], kvbuf_v.at[seq, :, :, col_half], partner)
    kv_cross.start()
    q_cross = remote(qstage_v, q_v.at[:, col_half], partner)
    q_cross.start()
    kv_own = local(stage_v.at[:, own_keys], kvbuf_v.at[seq, :, :, col_half])
    q_own = local(qstage_v, q_v.at[:, col_half])

    b_one = []
    for k in (1, 2, 3):
        to_z = around(zz, k)
        b_one.append(
            [
                remote(kvs_v.at[y4 * 4 + to_z, high], bufb_v.at[y4, zh, :, col_half], dev(z_=to_z))
                for y4 in range(4)
            ]
        )
    for copies in b_one:
        for copy in copies:
            copy.start()
    b_own = [local(kvs_v.at[y4 * 4 + zz, high], bufb_v.at[y4, zh, :, col_half]) for y4 in range(4)]

    load_wi.wait()

    @pl.loop(0, 4)
    def _(step):
        rows = pl.ds(pl.multiple_of(step * 256, 256), 256)
        hidden = jnp.dot(nm_v[rows, :], wi_v[...], preferred_element_type=F32)
        hid_v[rows, :] = (0.5 * hidden * (1.0 + lax.erf(hidden * (0.5**0.5)))).astype(BF16)

    kv_own.wait()
    kv_cross.wait_recv()

    def kv_send(slot, device):
        return pltpu.make_async_remote_copy(
            src_ref=kvbuf_v.at[slot],
            dst_ref=kvbuf_v.at[slot],
            send_sem=kvs_sem.at[slot],
            recv_sem=kvr_sem.at[slot],
            device_id=device,
            device_id_type=MESH,
        )

    def kv_out(slot, device, index):
        return pltpu.make_async_remote_copy(
            src_ref=kvbuf_v.at[slot],
            dst_ref=kvbuf_v.at[slot],
            send_sem=kvs_sem.at[8 + index],
            recv_sem=kvr_sem.at[slot],
            device_id=device,
            device_id_type=MESH,
        )

    for k in (1, 2, 3):
        pl.when(xx + k < 4)(kv_out(seq, dev(x_=lax.rem(xx + k, 4)), k).start)
    pl.when(core == 0)(kv_out(seq, twin, 0).start)

    load_w2.wait()

    @pl.loop(0, 4)
    def _(step):
        rows = pl.ds(pl.multiple_of(step * 256, 256), 256)
        part_v[rows, :] = jnp.dot(hid_v[rows, :], w2_v[...], preferred_element_type=F32).astype(BF16)

    acc_v[...] = jnp.zeros_like(acc_v)
    stat_v[0:1, :] = jnp.full((1, 1024), LOW, F32)
    stat_v[1:2, :] = jnp.zeros((1, 1024), F32)

    def attend(slot):
        keys = kvbuf_v[slot, 0]
        vals = kvbuf_v[slot, 1]
        vals_t = vals.T
        key_ids = slot * 1024 + half * 512 + lax.broadcasted_iota(jnp.int32, (512, 1), 0)

        @pl.loop(0, 4)
        def _(step):
            cols = pl.ds(pl.multiple_of(step * 256, 256), 256)
            scores = lax.dot_general(keys, q_v[cols, :], TT, preferred_element_type=F32)
            query_ids = seq * 1024 + step * 256 + lax.broadcasted_iota(jnp.int32, (1, 256), 1)
            allowed = (key_ids >= first_ref[:, cols]) & (key_ids <= query_ids)
            scores = jnp.where(allowed, scores, MASKED)
            old_max = stat_v[0:1, cols]
            new_max = jnp.maximum(old_max, jnp.max(scores, axis=0, keepdims=True))
            weights = jnp.exp(scores - new_max)
            keep = jnp.exp(old_max - new_max)
            stat_v[0:1, cols] = new_max
            stat_v[1:2, cols] = stat_v[1:2, cols] * keep + jnp.sum(weights, axis=0, keepdims=True)
            acc_v[:, cols] = acc_v[:, cols] * keep + jnp.dot(
                vals_t, weights.astype(BF16), preferred_element_type=F32
            )

    q_own.wait()
    q_cross.wait_recv()
    attend(seq)

    a_own.wait()
    for copy in a_one:
        copy.wait_recv()
    a_two = []
    for k in (1, 2, 3):
        to_z = around(zz, k)
        a_two.append(remote(bufa_v.at[:, to_z], kvx_v.at[:, zh, low, col_half], dev(z_=to_z)))
        a_two[-1].start()
    a_two_own = local(bufa_v.at[:, zz], kvx_v.at[:, zh, low, col_half])
    for copy in b_own:
        copy.wait()
    for copies in b_one:
        for copy in copies:
            copy.wait_recv()
    b_two = []
    for k in (1, 2, 3):
        to_y = around(yy, k)
        b_two.append(remote(bufb_v.at[to_y], kvx_v.at[yy, :, high, :], dev(y_=to_y)))
        b_two[-1].start()
    b_two_own = local(bufb_v.at[yy], kvx_v.at[yy, :, high, :])

    @pl.when(core == 1)
    def _():
        kv_send(seq - 1, twin).wait_recv()
        attend(seq - 1)

    @pl.loop(0, xx)
    def _(step):
        base = 2 * (xx - 1 - step)
        kv_send(base + core, twin).wait_recv()
        kv_send(base + core, twin).start()
        attend(base + core)
        kv_send(base + 1 - core, twin).wait_recv()
        attend(base + 1 - core)

    mine_v[...] = stat_v[...]
    stat_cross = remote(mine_v, theirs_v, partner)
    stat_cross.start()
    load_wo.wait()
    wo_cross.wait_recv()
    wo_twin = remote(wo_v.at[pl.ds(pl.multiple_of((1 - half) * 128 + core * 64, 64), 64), :],
                     wo_v.at[pl.ds(pl.multiple_of((1 - half) * 128 + core * 64, 64), 64), :], twin)
    wo_twin.start()
    wo_twin.wait_recv()
    stat_cross.wait_recv()
    top = jnp.maximum(stat_v[0:1, :], theirs_v[0:1, :])
    mine = jnp.exp(stat_v[0:1, :] - top)
    total = stat_v[1:2, :] * mine + theirs_v[1:2, :] * jnp.exp(theirs_v[0:1, :] - top)
    stat_v[0:1, :] = mine / total

    @pl.loop(0, 4)
    def _(step):
        cols = pl.ds(pl.multiple_of(step * 256, 256), 256)
        attended = (acc_v[:, cols] * stat_v[0:1, cols]).astype(BF16)
        summed = lax.dot_general(attended, wo_v[...], FF, preferred_element_type=F32)
        part_v[cols, :] = (part_v[cols, :].astype(F32) + summed).astype(BF16)

    def cols_of(which):
        return pl.ds(which * 1024, 1024)

    def axis_dev(which, step, first):
        along_y = (which == 0) == first
        return dev(y_=around(yy, step)) if along_y else dev(z_=around(zz, step))

    def scatter(which, first, source, size, direct, relay, sums, merged):
        pos = yy if (which == 0) == first else zz
        hs = size // 2

        def piece(step, part):
            begin = around(pos, step) * size + part * hs
            return source(pl.ds(pl.multiple_of(begin, hs), hs))

        plus = axis_dev(which, 1, first)
        minus = axis_dev(which, -1, first)
        r0 = remote(piece(2, 0), relay.at[which, 0], plus)
        r1 = remote(piece(2, 1), relay.at[which, 1], minus)
        d0 = remote(piece(1, 1), direct.at[which, 0], plus)
        d1 = remote(piece(-1, 0), direct.at[which, 1], minus)
        m0 = remote(sums.at[which, 0], merged.at[which, 0], plus)
        m1 = remote(sums.at[which, 1], merged.at[which, 1], minus)

        def one():
            for copy in (r0, r1, d0, d1):
                copy.start()

        def two():
            r0.wait_recv()
            sums[which, 0] = (piece(1, 0)[...].astype(F32) + relay[which, 0].astype(F32)).astype(BF16)
            m0.start()
            r1.wait_recv()
            sums[which, 1] = (piece(-1, 1)[...].astype(F32) + relay[which, 1].astype(F32)).astype(BF16)
            m1.start()

        def three():
            d0.wait_recv()
            d1.wait_recv()
            m0.wait_recv()
            m1.wait_recv()
            lower = piece(0, 0)[...].astype(F32) + direct[which, 1].astype(F32) + merged[which, 0].astype(F32)
            upper = piece(0, 1)[...].astype(F32) + direct[which, 0].astype(F32) + merged[which, 1].astype(F32)
            return lower, upper

        return one, two, three

    first_stage = [
        scatter(w, True, lambda rows, w=w: part_v.at[rows, cols_of(w)], 256, direct_v, relay_v, sums_v, merged_v)
        for w in (0, 1)
    ]
    second_stage = [
        scatter(w, False, lambda rows, w=w: fold_v.at[w, rows], 64, direct2_v, relay2_v, sums2_v, merged2_v)
        for w in (0, 1)
    ]
    for stage in first_stage:
        stage[0]()
    for stage in first_stage:
        stage[1]()
    for w in (0, 1):
        lower, upper = first_stage[w][2]()
        fold_v[w, 0:128] = lower.astype(BF16)
        fold_v[w, 128:256] = upper.astype(BF16)
        second_stage[w][0]()
    for stage in second_stage:
        stage[1]()

    base_of = (yy * 256, zz * 256)
    small_of = (zz, yy)

    def gather(which, first, base, size):
        pos = yy if (which == 0) == first else zz
        hs = size // 2

        def rows_at(step, part=None):
            begin = base + around(pos, step) * size
            if part is None:
                return na_v.at[pl.ds(pl.multiple_of(begin, size), size), cols_of(which)]
            return na_v.at[pl.ds(pl.multiple_of(begin + part * hs, hs), hs), cols_of(which)]

        plus = axis_dev(which, 1, first)
        minus = axis_dev(which, -1, first)
        own = rows_at(0)
        g0 = remote(own, own, plus)
        g1 = remote(own, own, minus)
        f0 = remote(rows_at(-1, 0), rows_at(-1, 0), plus)
        f1 = remote(rows_at(1, 1), rows_at(1, 1), minus)

        def one():
            g0.start()
            g1.start()

        def two():
            g0.wait_recv()
            f0.start()
            g1.wait_recv()
            f1.start()

        def three():
            f0.wait_recv()
            f1.wait_recv()

        return one, two, three

    small_gather = [gather(w, False, base_of[w], 64) for w in (0, 1)]
    large_gather = [gather(w, True, 0, 256) for w in (0, 1)]
    for w in (0, 1):
        lower, upper = second_stage[w][2]()
        begin = base_of[w] + small_of[w] * 64
        for part, value in ((0, lower), (1, upper)):
            rows = pl.ds(pl.multiple_of(begin + part * 32, 32), 32)
            na_v[rows, cols_of(w)] = (x_v[rows, cols_of(w)].astype(F32) + value).astype(BF16)
        small_gather[w][0]()

    a_two_own.wait()
    b_two_own.wait()
    for copy in a_two + b_two:
        copy.wait_recv()
    x_copies = []
    for k in range(1, 8):
        to = lax.rem(seq + k, 8)
        x_copies.append(remote(kvx_v.at[to // 2, lax.rem(to, 2)], kvout_hbm.at[seq], (to, ten)))
        x_copies[-1].start()
    x_own = local(kvx_v.at[xx, core], kvout_hbm.at[seq])

    for stage in small_gather:
        stage[1]()
    for w in (0, 1):
        small_gather[w][2]()
        large_gather[w][0]()
    for stage in large_gather:
        stage[1]()
    for stage in large_gather:
        stage[2]()
    out_copy = local(na_v, out_hbm)
    x_own.wait()
    for copy in x_copies:
        copy.wait_recv()
    out_copy.wait()
    for copy in pending:
        copy.wait_send()
    for k in (1, 2, 3):
        pl.when(xx + k < 4)(kv_out(seq, dev(x_=lax.rem(xx + k, 4)), k).wait_send)
    pl.when(core == 0)(kv_out(seq, twin, 0).wait_send)

    @pl.loop(0, xx)
    def _(step):
        base = 2 * (xx - 1 - step)
        kv_send(base + core, twin).wait_send()


def on_device(
    hidden_in,
    gain_attn,
    gain_mlp,
    w_qkv,
    w_attn_out,
    w_mlp_in,
    w_mlp_out,
    segment_ids,
    positions,
    kv_prefill,
    page_source,
):
    seq = lax.axis_index("seq")
    half = lax.rem(lax.axis_index("tensor"), 2)
    lane = jnp.arange(128, dtype=jnp.int32)[None, :]
    rot_dims = HD // 4
    freqs = 10000.0 ** (-((lane % (rot_dims // 2)).astype(F32) * 2.0 / rot_dims))
    angles = positions.astype(F32)[:, None] * freqs
    turns = (lane < rot_dims) & (half == 0)
    cosine = jnp.where(turns, jnp.cos(angles), 1.0)
    sine = jnp.where(turns, jnp.sin(angles) * jnp.where(lane < rot_dims // 2, -1.0, 1.0), 0.0)
    token_ids = seq * 1024 + jnp.arange(1024, dtype=jnp.int32)
    first = jnp.where(segment_ids == 0, 0, token_ids - positions)[None, :]
    vmem = pl.BlockSpec(memory_space=pltpu.VMEM)
    hbm = pl.BlockSpec(memory_space=pl.ANY)
    smem = pl.BlockSpec(memory_space=pltpu.SMEM)
    out, pages = pl.pallas_call(
        layer_kernel,
        name="layer",
        out_shape=(
            jax.ShapeDtypeStruct((1024, 2048), BF16),
            jax.ShapeDtypeStruct((8, 1024, 256), BF16),
        ),
        in_specs=[hbm, vmem, vmem, hbm, hbm, hbm, hbm, vmem, vmem, vmem, smem, hbm],
        out_specs=(hbm, hbm),
        scratch_shapes=[
            pltpu.VMEM((1024, 2048), BF16),
            pltpu.VMEM((1024, 2048), BF16),
            pltpu.VMEM((1024, 2048), BF16),
            pltpu.VMEM((2048, 384), BF16),
            pltpu.VMEM((2048, 512), BF16),
            pltpu.VMEM((512, 2048), BF16),
            pltpu.VMEM((256, 2048), BF16),
            pltpu.VMEM((1024, 512), BF16),
            pltpu.VMEM((1024, 2048), BF16),
            pltpu.VMEM((16, 1024, 128), BF16),
            pltpu.VMEM((16, 1024, 128), BF16),
            pltpu.VMEM((4, 4, 512, 128), BF16),
            pltpu.VMEM((4, 2, 512, 256), BF16),
            pltpu.VMEM((4, 2, 1024, 256), BF16),
            pltpu.VMEM((8, 2, 512, 256), BF16),
            pltpu.VMEM((2, 1024, 128), BF16),
            pltpu.VMEM((1024, 128), BF16),
            pltpu.VMEM((1024, 256), BF16),
            pltpu.VMEM((256, 1024), F32),
            pltpu.VMEM((8, 1024), F32),
            pltpu.VMEM((8, 1024), F32),
            pltpu.VMEM((8, 1024), F32),
            pltpu.VMEM((2, 2, 128, 1024), BF16),
            pltpu.VMEM((2, 2, 128, 1024), BF16),
            pltpu.VMEM((2, 2, 128, 1024), BF16),
            pltpu.VMEM((2, 2, 128, 1024), BF16),
            pltpu.VMEM((2, 256, 1024), BF16),
            pltpu.VMEM((2, 2, 32, 1024), BF16),
            pltpu.VMEM((2, 2, 32, 1024), BF16),
            pltpu.VMEM((2, 2, 32, 1024), BF16),
            pltpu.VMEM((2, 2, 32, 1024), BF16),
            pltpu.SemaphoreType.DMA((24,)),
            pltpu.SemaphoreType.DMA((80,)),
            pltpu.SemaphoreType.DMA((80,)),
            pltpu.SemaphoreType.DMA((12,)),
            pltpu.SemaphoreType.DMA((8,)),
        ],
        compiler_params=pltpu.CompilerParams(
            collective_id=0, has_side_effects=True, vmem_limit_bytes=67043328
        ),
    )(
        hidden_in,
        gain_attn[None, :],
        gain_mlp[None, :],
        w_qkv,
        w_attn_out,
        w_mlp_in,
        w_mlp_out,
        cosine,
        sine,
        first,
        page_source,
        kv_prefill.reshape(16, 1024, 128),
    )
    return (out, pages.reshape(8, 8, 2, 64, 256))


def solution(mesh):
    placed = (
        P("seq", None),
        P(),
        P(),
        P(None, None, "tensor"),
        P("tensor", None),
        P(None, "tensor"),
        P("tensor", None),
        P("seq"),
        P("seq"),
        P("seq", None, None, None, "tensor"),
        P(),
    )
    return jax.shard_map(
        on_device,
        mesh=mesh,
        in_specs=placed,
        out_specs=(P("seq", None), P("tensor", None, None, None, "seq")),
        check_vma=False,
    )
```

time: 332 us -> 163 us (0.49)
  the two profiles are of different devices: /device:TPU:6 before, /device:TPU:1 now
where the time goes in v1:
time: 163 us
  Pallas kernels  151 us (93%)
  local copies, waits for them, and re-layouts  6.96 us (4%)
  other arithmetic  4.45 us (3%)
    pallas_call x1, Pallas kernels, on_device(): pl.pallas_call(layer_kernel, name='layer', out_shape=(jax.ShapeDtypeStruc...  151 us
    unnamed x4, local copies, waits for them, and re-layouts  6.96 us

profile of v1, /device:TPU:1, one launch (start us, length us, event | category | flops | bytes accessed | tf_op | source)
XLA Modules:
  0.0 162.7 jit_solution(12284485997484025349)
XLA Ops:
  0.7 1.4 subtract_select_fusion
  2.0 3.1 %fusion.2 = (f32[1024,128]{1,0:T(8,128)}, f32[1024,128]{1,0:T(8,128)}) fusion(f32[128]{0:T(128)S(1)} %get-tuple-element.10, f32[128]{0:T(128)S(1)} %get-tuple-element.11, f32[1024]{0:T(1024)S(1)} %get-tuple-element.9, pred[128]{0:T(512)(128)(4,1)S(1)} %compare_and_fusion), kind=kLoop, calls=%fused_computation.4 | loop fusion | flops 524288 | bytes 1053824 | tf_op jit(solution)/shard_map/jit(_where)/select_n | solution.py:511
  5.1 150.6 %layer.1 = (bf16[1024,2048]{1,0:T(8,128)(2,1)}, bf16[8,1024,256]{2,1,0:T(8,128)(2,1)}) custom-call(bf16[1024,2048]{1,0:T(8,128)(2,1)} %x_hbm.1, f32[1,2048]{1,0:T(1,128)} %bitcast.8, f32[1,2048]{1,0:T(1,128)} %bitcast.9, bf16[3,2048,128]{2,1,0:T(8,128)(2,1)} %wqkv_hbm.1, bf16[128,2048]{1,0:T(8,128)(2,1)} %wo_hbm.1, bf16[2048,512]{1,0:T(8,128)(2,1)} %wi_hbm.1, ...), custom_call_target="tpu_custom_call" | custom-call | tf_op jit(solution)/shard_map/layer/pallas_call | solution.py:517
  155.7 0.0 copy-start
  155.7 4.9 %copy.15 = bf16[1024,2048]{1,0:T(8,128)(2,1)} copy(bf16[1024,2048]{1,0:T(8,128)(2,1)} %get-tuple-element.14) | data formatting | bytes 8388608
  160.7 0.0 copy-done
  160.7 2.0 %copy.16 = bf16[8,8,2,64,256]{4,3,2,1,0:T(8,128)(2,1)} copy(bf16[8,8,2,64,256]{4,3,2,1,0:T(8,128)(2,1)S(1)} %bitcast.6) | data formatting | bytes 8388608
  (2 shorter events, 0.0 us)
Async XLA Ops:
  155.7 5.0 %copy-start = (bf16[8,1024,256]{2,1,0:T(8,128)(2,1)S(1)}, bf16[8,1024,256]{2,1,0:T(8,128)(2,1)}, u32[]{:S(2)}) copy-start(bf16[8,1024,256]{2,1,0:T(8,128)(2,1)} %get-tuple-element.5) | copy-start | bytes 12582916

commit v2 on v1

--- a/solution.py
+++ b/solution.py
@@ -1,5 +1,6 @@
 import jax
 import jax.numpy as jnp
+import numpy as np
 from jax import lax
 from jax.experimental import pallas as pl
 from jax.experimental.pallas import tpu as pltpu
@@ -23,9 +24,9 @@
     wo_hbm,
     wi_hbm,
     w2_hbm,
-    cos_ref,
-    sin_ref,
-    first_ref,
+    freq_ref,
+    seg_ref,
+    pos_ref,
     psrc_ref,
     kv_hbm,
     out_hbm,
@@ -49,6 +50,7 @@
     qstage_v,
     q_v,
     acc_v,
+    att_v,
     stat_v,
     mine_v,
     theirs_v,
@@ -61,6 +63,9 @@
     relay2_v,
     sums2_v,
     merged2_v,
+    cos_v,
+    sin_v,
+    first_v,
     lsem,
     ssem,
     rsem,
@@ -112,20 +117,27 @@
         copy.start()
         return copy
 
-    load_x = local(x_hbm, x_v)
-    load_w = [local(wqkv_hbm.at[c], wcat_v.at[:, pl.ds(j * 128, 128)]) for j, c in ((0, 1), (1, 2), (2, 0))]
-    load_kv = local(kv_hbm, kvin_v)
-    load_wi = local(wi_hbm, wi_v)
-    load_w2 = local(w2_hbm, w2_v)
-    own_rows = pl.ds(pl.multiple_of(half * 128, 128), 128)
-    load_wo = local(wo_hbm, wo_v.at[own_rows, :])
-
     barrier = pltpu.get_barrier_semaphore()
     peers = [dev(y_=around(yy, k)) for k in (1, 2, 3)]
     peers += [dev(z_=around(zz, k)) for k in (1, 2, 3)]
     peers += [(lax.rem(seq + k, 8), ten) for k in range(1, 8)]
     for peer in peers:
         pl.semaphore_signal(barrier, inc=1, device_id=peer, device_id_type=MESH)
+
+    load_kv = local(kv_hbm, kvin_v)
+    load_x = local(x_hbm, x_v)
+    load_w = [local(wqkv_hbm.at[c], wcat_v.at[:, pl.ds(j * 128, 128)]) for j, c in ((0, 1), (1, 2), (2, 0))]
+    load_wi = local(wi_hbm, wi_v)
+    load_w2 = local(w2_hbm, w2_v)
+    own_rows = pl.ds(pl.multiple_of(half * 128, 128), 128)
+    load_wo = local(wo_hbm, wo_v.at[own_rows, :])
+
+    load_kv.wait()
+
+    @pl.loop(0, 16)
+    def _(group):
+        kvs_v[group] = kvin_v[lax.rem(psrc_ref[group * 8 + seq], 16)]
+
     pl.semaphore_wait(barrier, len(peers))
 
     partner = dev(z_=zz + 1 - 2 * half)
@@ -135,21 +147,84 @@
     wo_cross = remote(wo_hbm.at[pl.ds(pl.multiple_of(core * 64, 64), 64)], wo_v.at[half_rows, :], partner)
     wo_cross.start()
 
-    load_kv.wait()
-
-    @pl.loop(0, 16)
-    def _(group):
-        kvs_v[group] = kvin_v[lax.rem(psrc_ref[group * 8 + seq], 16)]
-
-    low = pl.ds(0, 512)
-    high = pl.ds(512, 512)
     col_half = pl.ds(pl.multiple_of(half * 128, 128), 128)
-    a_one = []
-    for k in (1, 2, 3):
-        to_y = around(yy, k)
-        a_one.append(remote(kvs_v.at[pl.ds(to_y * 4, 4), low], bufa_v.at[yy], dev(y_=to_y)))
-        a_one[-1].start()
-    a_own = local(kvs_v.at[pl.ds(yy * 4, 4), low], bufa_v.at[yy])
+
+    def low(part):
+        return pl.ds(part * 256, 256)
+
+    def high(part):
+        return pl.ds(512 + part * 256, 256)
+
+    def y_first(part):
+        copies = [
+            remote(kvs_v.at[pl.ds(around(yy, k) * 4, 4), low(part)], bufa_v.at[part, yy], dev(y_=around(yy, k)))
+            for k in (1, 3, 2)
+        ]
+        for copy in copies:
+            copy.start()
+        return copies, [local(kvs_v.at[pl.ds(yy * 4, 4), low(part)], bufa_v.at[part, yy])]
+
+    def then_z(part):
+        copies = [
+            remote(bufa_v.at[part, :, around(zz, k)], kvx_v.at[:, zh, low(part), col_half], dev(z_=around(zz, k)))
+            for k in (1, 3, 2)
+        ]
+        for copy in copies:
+            copy.start()
+        return copies, [local(bufa_v.at[part, :, zz], kvx_v.at[:, zh, low(part), col_half])]
+
+    def z_first(part):
+        copies = [
+            remote(
+                kvs_v.at[y4 * 4 + around(zz, k), high(part)],
+                bufb_v.at[part, y4, zh, :, col_half],
+                dev(z_=around(zz, k)),
+            )
+            for k in (1, 3, 2)
+            for y4 in range(4)
+        ]
+        for copy in copies:
+            copy.start()
+        own = [local(kvs_v.at[y4 * 4 + zz, high(part)], bufb_v.at[part, y4, zh, :, col_half]) for y4 in range(4)]
+        return copies, own
+
+    def then_y(part):
+        copies = [
+            remote(bufb_v.at[part, around(yy, k)], kvx_v.at[yy, :, high(part), :], dev(y_=around(yy, k)))
+            for k in (1, 3, 2)
+        ]
+        for copy in copies:
+            copy.start()
+        return copies, [local(bufb_v.at[part, yy], kvx_v.at[yy, :, high(part), :])]
+
+    def along_x(rows):
+        copies = []
+        for k in (1, 2, 7, 6, 3, 5, 4):
+            to = lax.rem(seq + k, 8)
+            copies.append(
+                remote(kvx_v.at[to // 2, lax.rem(to, 2), rows], kvout_hbm.at[seq, rows], (to, ten))
+            )
+            copies[-1].start()
+        return copies, [local(kvx_v.at[xx, core, rows], kvout_hbm.at[seq, rows])]
+
+    def arrived(stage):
+        copies, own = stage
+        for copy in own:
+            copy.wait()
+        for copy in copies:
+            copy.wait_recv()
+
+    y_one = [y_first(0), y_first(1)]
+
+    positions = pos_ref[...]
+    angles = freq_ref[:, 0:1] * positions.astype(F32)
+    turn = jnp.broadcast_to(half, (32, 1024)) == 0
+    cosine = jnp.where(turn, jnp.cos(angles), 1.0)
+    sine = jnp.where(turn, jnp.sin(angles), 0.0)
+    cos_v[...] = jnp.concatenate([cosine, cosine, jnp.ones((64, 1024), F32)], axis=0).T
+    sin_v[...] = jnp.concatenate([-sine, sine, jnp.zeros((64, 1024), F32)], axis=0).T
+    tokens = seq * 1024 + lax.broadcasted_iota(jnp.int32, (1, 1024), 1)
+    first_v[...] = jnp.where(seg_ref[...] == 0, 0, tokens - positions)
 
     load_x.wait()
     for copy in load_w:
@@ -172,8 +247,8 @@
         kv = jnp.dot(na, wcat_v[:, 0:256], preferred_element_type=F32)
         q = jnp.dot(na, wcat_v[:, 256:384], preferred_element_type=F32)
         lanes = lax.broadcasted_iota(jnp.int32, (256, 128), 1)
-        cosine = cos_ref[rows, :]
-        sine = sin_ref[rows, :]
+        cosine = cos_v[rows, :]
+        sine = sin_v[rows, :]
 
         def turned(values_in):
             other = jnp.where(lanes < 32, pltpu.roll(values_in, 96, 1), pltpu.roll(values_in, 32, 1))
@@ -192,19 +267,7 @@
     kv_own = local(stage_v.at[:, own_keys], kvbuf_v.at[seq, :, :, col_half])
     q_own = local(qstage_v, q_v.at[:, col_half])
 
-    b_one = []
-    for k in (1, 2, 3):
-        to_z = around(zz, k)
-        b_one.append(
-            [
-                remote(kvs_v.at[y4 * 4 + to_z, high], bufb_v.at[y4, zh, :, col_half], dev(z_=to_z))
-                for y4 in range(4)
-            ]
-        )
-    for copies in b_one:
-        for copy in copies:
-            copy.start()
-    b_own = [local(kvs_v.at[y4 * 4 + zz, high], bufb_v.at[y4, zh, :, col_half]) for y4 in range(4)]
+    z_one = [z_first(0), z_first(1)]
 
     load_wi.wait()
 
@@ -217,29 +280,52 @@
     kv_own.wait()
     kv_cross.wait_recv()
 
-    def kv_send(slot, device):
+    def kv_part(slot, part, device, index):
+        return pltpu.make_async_remote_copy(
+            src_ref=kvbuf_v.at[slot, part],
+            dst_ref=kvbuf_v.at[slot, part],
+            send_sem=kvs_sem.at[index],
+            recv_sem=kvr_sem.at[slot, part],
+            device_id=device,
+            device_id_type=MESH,
+        )
+
+    def kv_twin(slot):
         return pltpu.make_async_remote_copy(
             src_ref=kvbuf_v.at[slot],
             dst_ref=kvbuf_v.at[slot],
-            send_sem=kvs_sem.at[slot],
-            recv_sem=kvr_sem.at[slot],
-            device_id=device,
+            send_sem=kvs_sem.at[8 + slot],
+            recv_sem=kvr_sem.at[slot, 2],
+            device_id=twin,
             device_id_type=MESH,
         )
 
-    def kv_out(slot, device, index):
-        return pltpu.make_async_remote_copy(
-            src_ref=kvbuf_v.at[slot],
-            dst_ref=kvbuf_v.at[slot],
-            send_sem=kvs_sem.at[8 + index],
-            recv_sem=kvr_sem.at[slot],
-            device_id=device,
-            device_id_type=MESH,
-        )
-
-    for k in (1, 2, 3):
-        pl.when(xx + k < 4)(kv_out(seq, dev(x_=lax.rem(xx + k, 4)), k).start)
-    pl.when(core == 0)(kv_out(seq, twin, 0).start)
+    def sends(copies):
+        def start():
+            for copy in copies:
+                copy.start()
+
+        def wait():
+            for copy in copies:
+                copy.wait_send()
+
+        return start, wait
+
+    chips = [dev(x_=k) for k in range(4)]
+    own_out = [
+        sends([kv_part(seq, 1, chips[3], 0), kv_part(seq, 0, chips[1], 1), kv_part(seq, 1, chips[1], 2), kv_part(seq, 0, chips[3], 3)]),
+        sends([kv_part(seq, 1, chips[0], 0), kv_part(seq, 0, chips[2], 1), kv_part(seq, 1, chips[2], 2)]),
+        sends([kv_part(seq, 0, chips[3], 0), kv_part(seq, 1, chips[3], 1)]),
+    ]
+    passed_on = [
+        kv_part(2 + core, 1, chips[3], 4),
+        kv_part(core, 0, chips[2], 4),
+        kv_part(2 + core, 0, chips[3], 4),
+        kv_part(core, 1, chips[2], 4),
+    ]
+    for k in range(3):
+        pl.when(xx == k)(own_out[k][0])
+    pl.when(core == 0)(kv_twin(seq).start)
 
     load_w2.wait()
 
@@ -247,6 +333,11 @@
     def _(step):
         rows = pl.ds(pl.multiple_of(step * 256, 256), 256)
         part_v[rows, :] = jnp.dot(hid_v[rows, :], w2_v[...], preferred_element_type=F32).astype(BF16)
+
+    z_two = []
+    for part in (0, 1):
+        arrived(y_one[part])
+        z_two.append(then_z(part))
 
     acc_v[...] = jnp.zeros_like(acc_v)
     stat_v[0:1, :] = jnp.full((1, 1024), LOW, F32)
@@ -263,7 +354,7 @@
             cols = pl.ds(pl.multiple_of(step * 256, 256), 256)
             scores = lax.dot_general(keys, q_v[cols, :], TT, preferred_element_type=F32)
             query_ids = seq * 1024 + step * 256 + lax.broadcasted_iota(jnp.int32, (1, 256), 1)
-            allowed = (key_ids >= first_ref[:, cols]) & (key_ids <= query_ids)
+            allowed = (key_ids >= first_v[:, cols]) & (key_ids <= query_ids)
             scores = jnp.where(allowed, scores, MASKED)
             old_max = stat_v[0:1, cols]
             new_max = jnp.maximum(old_max, jnp.max(scores, axis=0, keepdims=True))
@@ -279,39 +370,32 @@
     q_cross.wait_recv()
     attend(seq)
 
-    a_own.wait()
-    for copy in a_one:
-        copy.wait_recv()
-    a_two = []
-    for k in (1, 2, 3):
-        to_z = around(zz, k)
-        a_two.append(remote(bufa_v.at[:, to_z], kvx_v.at[:, zh, low, col_half], dev(z_=to_z)))
-        a_two[-1].start()
-    a_two_own = local(bufa_v.at[:, zz], kvx_v.at[:, zh, low, col_half])
-    for copy in b_own:
-        copy.wait()
-    for copies in b_one:
-        for copy in copies:
-            copy.wait_recv()
-    b_two = []
-    for k in (1, 2, 3):
-        to_y = around(yy, k)
-        b_two.append(remote(bufb_v.at[to_y], kvx_v.at[yy, :, high, :], dev(y_=to_y)))
-        b_two[-1].start()
-    b_two_own = local(bufb_v.at[yy], kvx_v.at[yy, :, high, :])
+    for k in range(4):
+
+        @pl.when(xx == k)
+        def _(k=k):
+            passed_on[k].wait_recv()
+            passed_on[k].start()
+
+    arrived(z_one[0])
+    y_two = [then_y(0)]
 
     @pl.when(core == 1)
     def _():
-        kv_send(seq - 1, twin).wait_recv()
+        kv_twin(seq - 1).wait_recv()
         attend(seq - 1)
+
+    arrived(z_one[1])
+    y_two.append(then_y(1))
 
     @pl.loop(0, xx)
     def _(step):
         base = 2 * (xx - 1 - step)
-        kv_send(base + core, twin).wait_recv()
-        kv_send(base + core, twin).start()
+        pl.when(jnp.logical_or(step > 0, xx == 3))(kv_part(base + core, 0, twin, 0).wait_recv)
+        pl.when(jnp.logical_or(base > 0, xx < 3))(kv_part(base + core, 1, twin, 0).wait_recv)
+        kv_twin(base + core).start()
         attend(base + core)
-        kv_send(base + 1 - core, twin).wait_recv()
+        kv_twin(base + 1 - core).wait_recv()
         attend(base + 1 - core)
 
     mine_v[...] = stat_v[...]
@@ -329,22 +413,26 @@
     total = stat_v[1:2, :] * mine + theirs_v[1:2, :] * jnp.exp(theirs_v[0:1, :] - top)
     stat_v[0:1, :] = mine / total
 
-    @pl.loop(0, 4)
-    def _(step):
-        cols = pl.ds(pl.multiple_of(step * 256, 256), 256)
-        attended = (acc_v[:, cols] * stat_v[0:1, cols]).astype(BF16)
-        summed = lax.dot_general(attended, wo_v[...], FF, preferred_element_type=F32)
-        part_v[cols, :] = (part_v[cols, :].astype(F32) + summed).astype(BF16)
+    att_v[...] = (acc_v[...] * stat_v[0:1, :]).astype(BF16)
+
+    def project(group):
+        cols = cols_of(group)
+
+        @pl.loop(0, 4)
+        def _(step):
+            rows = pl.ds(pl.multiple_of(step * 256, 256), 256)
+            summed = lax.dot_general(att_v[:, rows], wo_v[:, cols], FF, preferred_element_type=F32)
+            part_v[rows, cols] = (part_v[rows, cols].astype(F32) + summed).astype(BF16)
 
     def cols_of(which):
-        return pl.ds(which * 1024, 1024)
+        return pl.ds(which * 512, 512)
 
     def axis_dev(which, step, first):
-        along_y = (which == 0) == first
+        along_y = (which % 2 == 0) == first
         return dev(y_=around(yy, step)) if along_y else dev(z_=around(zz, step))
 
     def scatter(which, first, source, size, direct, relay, sums, merged):
-        pos = yy if (which == 0) == first else zz
+        pos = yy if (which % 2 == 0) == first else zz
         hs = size // 2
 
         def piece(step, part):
@@ -383,31 +471,41 @@
 
         return one, two, three
 
+    groups = range(4)
     first_stage = [
         scatter(w, True, lambda rows, w=w: part_v.at[rows, cols_of(w)], 256, direct_v, relay_v, sums_v, merged_v)
-        for w in (0, 1)
+        for w in groups
     ]
     second_stage = [
         scatter(w, False, lambda rows, w=w: fold_v.at[w, rows], 64, direct2_v, relay2_v, sums2_v, merged2_v)
-        for w in (0, 1)
+        for w in groups
     ]
-    for stage in first_stage:
-        stage[0]()
-    for stage in first_stage:
-        stage[1]()
-    for w in (0, 1):
+    for w in groups:
+        project(w)
+        first_stage[w][0]()
+    arrived(y_two[0])
+    x_three = [along_x(high(0))]
+    for w in groups:
+        first_stage[w][1]()
+    arrived(z_two[0])
+    x_three.append(along_x(low(0)))
+    for w in groups:
         lower, upper = first_stage[w][2]()
         fold_v[w, 0:128] = lower.astype(BF16)
         fold_v[w, 128:256] = upper.astype(BF16)
         second_stage[w][0]()
-    for stage in second_stage:
-        stage[1]()
-
-    base_of = (yy * 256, zz * 256)
-    small_of = (zz, yy)
+    arrived(y_two[1])
+    x_three.append(along_x(high(1)))
+    arrived(z_two[1])
+    x_three.append(along_x(low(1)))
+    for w in groups:
+        second_stage[w][1]()
+
+    base_of = (yy * 256, zz * 256) * 2
+    small_of = (zz, yy) * 2
 
     def gather(which, first, base, size):
-        pos = yy if (which == 0) == first else zz
+        pos = yy if (which % 2 == 0) == first else zz
         hs = size // 2
 
         def rows_at(step, part=None):
@@ -440,51 +538,41 @@
 
         return one, two, three
 
-    small_gather = [gather(w, False, base_of[w], 64) for w in (0, 1)]
-    large_gather = [gather(w, True, 0, 256) for w in (0, 1)]
-    for w in (0, 1):
+    small_gather = [gather(w, False, base_of[w], 64) for w in groups]
+    large_gather = [gather(w, True, 0, 256) for w in groups]
+    for w in groups:
         lower, upper = second_stage[w][2]()
         begin = base_of[w] + small_of[w] * 64
         for part, value in ((0, lower), (1, upper)):
             rows = pl.ds(pl.multiple_of(begin + part * 32, 32), 32)
             na_v[rows, cols_of(w)] = (x_v[rows, cols_of(w)].astype(F32) + value).astype(BF16)
         small_gather[w][0]()
-
-    a_two_own.wait()
-    b_two_own.wait()
-    for copy in a_two + b_two:
-        copy.wait_recv()
-    x_copies = []
-    for k in range(1, 8):
-        to = lax.rem(seq + k, 8)
-        x_copies.append(remote(kvx_v.at[to // 2, lax.rem(to, 2)], kvout_hbm.at[seq], (to, ten)))
-        x_copies[-1].start()
-    x_own = local(kvx_v.at[xx, core], kvout_hbm.at[seq])
-
-    for stage in small_gather:
-        stage[1]()
-    for w in (0, 1):
+    for w in groups:
+        small_gather[w][1]()
+    for w in groups:
         small_gather[w][2]()
         large_gather[w][0]()
-    for stage in large_gather:
-        stage[1]()
-    for stage in large_gather:
-        stage[2]()
-    out_copy = local(na_v, out_hbm)
-    x_own.wait()
-    for copy in x_copies:
-        copy.wait_recv()
-    out_copy.wait()
+    for w in groups:
+        large_gather[w][1]()
+    for w in groups:
+        large_gather[w][2]()
+    out_copies = [local(na_v.at[pl.ds(k * 256, 256)], out_hbm.at[k]) for k in range(4)]
+    for stage in x_three:
+        arrived(stage)
+    for copy in out_copies:
+        copy.wait()
     for copy in pending:
         copy.wait_send()
-    for k in (1, 2, 3):
-        pl.when(xx + k < 4)(kv_out(seq, dev(x_=lax.rem(xx + k, 4)), k).wait_send)
-    pl.when(core == 0)(kv_out(seq, twin, 0).wait_send)
+    for k in range(3):
+        pl.when(xx == k)(own_out[k][1])
+    for k in range(4):
+        pl.when(xx == k)(passed_on[k].wait_send)
+    pl.when(core == 0)(kv_twin(seq).wait_send)
 
     @pl.loop(0, xx)
     def _(step):
         base = 2 * (xx - 1 - step)
-        kv_send(base + core, twin).wait_send()
+        kv_twin(base + core).wait_send()
 
 
 def on_device(
@@ -500,17 +588,10 @@
     kv_prefill,
     page_source,
 ):
-    seq = lax.axis_index("seq")
-    half = lax.rem(lax.axis_index("tensor"), 2)
-    lane = jnp.arange(128, dtype=jnp.int32)[None, :]
     rot_dims = HD // 4
-    freqs = 10000.0 ** (-((lane % (rot_dims // 2)).astype(F32) * 2.0 / rot_dims))
-    angles = positions.astype(F32)[:, None] * freqs
-    turns = (lane < rot_dims) & (half == 0)
-    cosine = jnp.where(turns, jnp.cos(angles), 1.0)
-    sine = jnp.where(turns, jnp.sin(angles) * jnp.where(lane < rot_dims // 2, -1.0, 1.0), 0.0)
-    token_ids = seq * 1024 + jnp.arange(1024, dtype=jnp.int32)
-    first = jnp.where(segment_ids == 0, 0, token_ids - positions)[None, :]
+    powers = np.arange(rot_dims // 2, dtype=np.float32) * np.float32(2.0) / np.float32(rot_dims)
+    freqs = np.power(np.float32(10000.0), -powers).astype(np.float32)
+    freqs = jnp.asarray(np.broadcast_to(freqs[:, None], (rot_dims // 2, 128)))
     vmem = pl.BlockSpec(memory_space=pltpu.VMEM)
     hbm = pl.BlockSpec(memory_space=pl.ANY)
     smem = pl.BlockSpec(memory_space=pltpu.SMEM)
@@ -518,7 +599,7 @@
         layer_kernel,
         name="layer",
         out_shape=(
-            jax.ShapeDtypeStruct((1024, 2048), BF16),
+            jax.ShapeDtypeStruct((4, 256, 2048), BF16),
             jax.ShapeDtypeStruct((8, 1024, 256), BF16),
         ),
         in_specs=[hbm, vmem, vmem, hbm, hbm, hbm, hbm, vmem, vmem, vmem, smem, hbm],
@@ -535,31 +616,35 @@
             pltpu.VMEM((1024, 2048), BF16),
             pltpu.VMEM((16, 1024, 128), BF16),
             pltpu.VMEM((16, 1024, 128), BF16),
-            pltpu.VMEM((4, 4, 512, 128), BF16),
-            pltpu.VMEM((4, 2, 512, 256), BF16),
+            pltpu.VMEM((2, 4, 4, 256, 128), BF16),
+            pltpu.VMEM((2, 4, 2, 256, 256), BF16),
             pltpu.VMEM((4, 2, 1024, 256), BF16),
             pltpu.VMEM((8, 2, 512, 256), BF16),
             pltpu.VMEM((2, 1024, 128), BF16),
             pltpu.VMEM((1024, 128), BF16),
             pltpu.VMEM((1024, 256), BF16),
             pltpu.VMEM((256, 1024), F32),
+            pltpu.VMEM((256, 1024), BF16),
             pltpu.VMEM((8, 1024), F32),
             pltpu.VMEM((8, 1024), F32),
             pltpu.VMEM((8, 1024), F32),
-            pltpu.VMEM((2, 2, 128, 1024), BF16),
-            pltpu.VMEM((2, 2, 128, 1024), BF16),
-            pltpu.VMEM((2, 2, 128, 1024), BF16),
-            pltpu.VMEM((2, 2, 128, 1024), BF16),
-            pltpu.VMEM((2, 256, 1024), BF16),
-            pltpu.VMEM((2, 2, 32, 1024), BF16),
-            pltpu.VMEM((2, 2, 32, 1024), BF16),
-            pltpu.VMEM((2, 2, 32, 1024), BF16),
-            pltpu.VMEM((2, 2, 32, 1024), BF16),
-            pltpu.SemaphoreType.DMA((24,)),
-            pltpu.SemaphoreType.DMA((80,)),
-            pltpu.SemaphoreType.DMA((80,)),
-            pltpu.SemaphoreType.DMA((12,)),
-            pltpu.SemaphoreType.DMA((8,)),
+            pltpu.VMEM((4, 2, 128, 512), BF16),
+            pltpu.VMEM((4, 2, 128, 512), BF16),
+            pltpu.VMEM((4, 2, 128, 512), BF16),
+            pltpu.VMEM((4, 2, 128, 512), BF16),
+            pltpu.VMEM((4, 256, 512), BF16),
+            pltpu.VMEM((4, 2, 32, 512), BF16),
+            pltpu.VMEM((4, 2, 32, 512), BF16),
+            pltpu.VMEM((4, 2, 32, 512), BF16),
+            pltpu.VMEM((4, 2, 32, 512), BF16),
+            pltpu.VMEM((1024, 128), F32),
+            pltpu.VMEM((1024, 128), F32),
+            pltpu.VMEM((1, 1024), jnp.int32),
+            pltpu.SemaphoreType.DMA((48,)),
+            pltpu.SemaphoreType.DMA((160,)),
+            pltpu.SemaphoreType.DMA((160,)),
+            pltpu.SemaphoreType.DMA((16,)),
+            pltpu.SemaphoreType.DMA((8, 3)),
         ],
         compiler_params=pltpu.CompilerParams(
             collective_id=0, has_side_effects=True, vmem_limit_bytes=67043328
@@ -572,13 +657,13 @@
         w_attn_out,
         w_mlp_in,
         w_mlp_out,
-        cosine,
-        sine,
-        first,
+        freqs,
+        segment_ids[None, :],
+        positions[None, :],
         page_source,
         kv_prefill.reshape(16, 1024, 128),
     )
-    return (out, pages.reshape(8, 8, 2, 64, 256))
+    return (out.reshape(1024, 2048), pages.reshape(8, 8, 2, 64, 256))
 
 
 def solution(mesh):

time: 163 us -> 140 us (0.86)
  the two profiles are of different devices: /device:TPU:1 before, /device:TPU:6 now
where the time goes in v2:
time: 140 us
  Pallas kernels  131 us (94%)
  local copies, waits for them, and re-layouts  8.29 us (6%)
    pallas_call x1, Pallas kernels, on_device(): pl.pallas_call(layer_kernel, name='layer', out_shape=(jax.ShapeDtypeStruc...  131 us
    unnamed x4, local copies, waits for them, and re-layouts  6.96 us

profile of v2, /device:TPU:6, one launch (start us, length us, event | category | flops | bytes accessed | tf_op | source)
XLA Modules:
  0.0 139.8 jit_solution(11955884425266172156)
XLA Ops:
  0.6 1.3 jit_solution_.3.freq_ref
  2.0 130.9 %layer.1 = (bf16[4,256,2048]{2,1,0:T(8,128)(2,1)}, bf16[8,1024,256]{2,1,0:T(8,128)(2,1)}) custom-call(bf16[1024,2048]{1,0:T(8,128)(2,1)} %x_hbm.1, f32[1,2048]{1,0:T(1,128)} %bitcast.10, f32[1,2048]{1,0:T(1,128)} %bitcast.11, bf16[3,2048,128]{2,1,0:T(8,128)(2,1)} %wqkv_hbm.1, bf16[128,2048]{1,0:T(8,128)(2,1)} %wo_hbm.1, bf16[2048,512]{1,0:T(8,128)(2,1)} %wi_hbm.1, ...), custom_call_target="tpu_custom_call" | custom-call | tf_op jit(solution)/shard_map/layer/pallas_call | solution.py:598
  132.8 0.0 copy-start
  132.9 4.9 %copy.16 = bf16[1024,2048]{1,0:T(8,128)(2,1)} copy(bf16[1024,2048]{1,0:T(8,128)(2,1)} %bitcast.8) | data formatting | bytes 8388608
  137.8 0.0 copy-done
  137.8 2.0 %copy.17 = bf16[8,8,2,64,256]{4,3,2,1,0:T(8,128)(2,1)} copy(bf16[8,8,2,64,256]{4,3,2,1,0:T(8,128)(2,1)S(1)} %bitcast.7) | data formatting | bytes 8388608
Async XLA Ops:
  132.8 5.0 %copy-start = (bf16[8,1024,256]{2,1,0:T(8,128)(2,1)S(1)}, bf16[8,1024,256]{2,1,0:T(8,128)(2,1)}, u32[]{:S(2)}) copy-start(bf16[8,1024,256]{2,1,0:T(8,128)(2,1)} %get-tuple-element.5) | copy-start | bytes 12582916

commit v3 on v2

--- a/solution.py
+++ b/solution.py
@@ -33,7 +33,6 @@
     kvout_hbm,
     x_v,
     na_v,
-    nm_v,
     wcat_v,
     wi_v,
     w2_v,
@@ -47,7 +46,6 @@
     kvx_v,
     kvbuf_v,
     stage_v,
-    qstage_v,
     q_v,
     acc_v,
     att_v,
@@ -126,7 +124,9 @@
 
     load_kv = local(kv_hbm, kvin_v)
     load_x = local(x_hbm, x_v)
-    load_w = [local(wqkv_hbm.at[c], wcat_v.at[:, pl.ds(j * 128, 128)]) for j, c in ((0, 1), (1, 2), (2, 0))]
+    q_cols = pl.ds(pl.multiple_of(256 + half * 128, 128), 128)
+    load_w = [local(wqkv_hbm.at[1], wcat_v.at[:, 0:128]), local(wqkv_hbm.at[2], wcat_v.at[:, 128:256])]
+    load_w.append(local(wqkv_hbm.at[0], wcat_v.at[:, q_cols]))
     load_wi = local(wi_hbm, wi_v)
     load_w2 = local(w2_hbm, w2_v)
     own_rows = pl.ds(pl.multiple_of(half * 128, 128), 128)
@@ -143,9 +143,19 @@
     partner = dev(z_=zz + 1 - 2 * half)
     twin = (seq + 1 - 2 * core, ten)
 
-    half_rows = pl.ds(pl.multiple_of(half * 128 + core * 64, 64), 64)
-    wo_cross = remote(wo_hbm.at[pl.ds(pl.multiple_of(core * 64, 64), 64)], wo_v.at[half_rows, :], partner)
-    wo_cross.start()
+    wo_piece = pl.ds(pl.multiple_of(seq * 16, 16), 16)
+    wq_piece = pl.ds(pl.multiple_of(seq * 256, 256), 256)
+    pair_weights = [
+        remote(wo_hbm.at[wo_piece], wo_v.at[pl.ds(pl.multiple_of(half * 128 + seq * 16, 16), 16)], partner),
+        remote(wqkv_hbm.at[0, wq_piece], wcat_v.at[wq_piece, q_cols], partner),
+    ]
+    for copy in pair_weights:
+        copy.start()
+    wo_here = wo_v.at[pl.ds(pl.multiple_of((1 - half) * 128 + seq * 16, 16), 16)]
+    wq_here = wcat_v.at[wq_piece, pl.ds(pl.multiple_of(256 + (1 - half) * 128, 128), 128)]
+    seq_weights = [
+        remote(piece, piece, (lax.rem(seq + k, 8), ten)) for piece in (wq_here, wo_here) for k in (1, 2, 7, 6, 3, 5, 4)
+    ]
 
     col_half = pl.ds(pl.multiple_of(half * 128, 128), 128)
 
@@ -173,20 +183,23 @@
             copy.start()
         return copies, [local(bufa_v.at[part, :, zz], kvx_v.at[:, zh, low(part), col_half])]
 
+    away = 2 * half - 1
+
     def z_first(part):
-        copies = [
-            remote(
-                kvs_v.at[y4 * 4 + around(zz, k), high(part)],
-                bufb_v.at[part, y4, zh, :, col_half],
-                dev(z_=around(zz, k)),
-            )
-            for k in (1, 3, 2)
-            for y4 in range(4)
+        return [
+            [
+                remote(
+                    kvs_v.at[y4 * 4 + around(zz, k), high(part)],
+                    bufb_v.at[part, y4, zh, :, col_half],
+                    dev(z_=around(zz, k)),
+                )
+                for y4 in range(4)
+            ]
+            for k in (away, -away, 2)
         ]
-        for copy in copies:
-            copy.start()
-        own = [local(kvs_v.at[y4 * 4 + zz, high(part)], bufb_v.at[part, y4, zh, :, col_half]) for y4 in range(4)]
-        return copies, own
+
+    def z_own(part):
+        return [local(kvs_v.at[y4 * 4 + zz, high(part)], bufb_v.at[part, y4, zh, :, col_half]) for y4 in range(4)]
 
     def then_y(part):
         copies = [
@@ -215,12 +228,16 @@
             copy.wait_recv()
 
     y_one = [y_first(0), y_first(1)]
+    z_sends = [z_first(0), z_first(1)]
+    for part in (0, 1):
+        for copy in z_sends[part][0]:
+            copy.start()
 
     positions = pos_ref[...]
-    angles = freq_ref[:, 0:1] * positions.astype(F32)
-    turn = jnp.broadcast_to(half, (32, 1024)) == 0
-    cosine = jnp.where(turn, jnp.cos(angles), 1.0)
-    sine = jnp.where(turn, jnp.sin(angles), 0.0)
+    freqs = jnp.broadcast_to(freq_ref[...], (128, 128)).T[0:32, 0:1]
+    angles = freqs * positions.astype(F32)
+    cosine = jnp.cos(angles)
+    sine = jnp.sin(angles)
     cos_v[...] = jnp.concatenate([cosine, cosine, jnp.ones((64, 1024), F32)], axis=0).T
     sin_v[...] = jnp.concatenate([-sine, sine, jnp.zeros((64, 1024), F32)], axis=0).T
     tokens = seq * 1024 + lax.broadcasted_iota(jnp.int32, (1, 1024), 1)
@@ -232,50 +249,60 @@
     ga = ga_ref[...]
     gm = gm_ref[...]
 
-    @pl.loop(0, 4)
-    def _(step):
-        start = lax.rem(step * 256 + (1 - half) * 512, 1024)
-        rows = pl.ds(pl.multiple_of(start, 256), 256)
+    def normed_rows(rows):
         values = x_v[rows, :].astype(F32)
         mean = jnp.mean(values, axis=-1, keepdims=True)
         centered = values - mean
         spread = jnp.mean(centered * centered, axis=-1, keepdims=True)
-        normed = centered * lax.rsqrt(spread + 1e-05)
-        na = (normed * ga).astype(BF16)
-        na_v[rows, :] = na
-        nm_v[rows, :] = (normed * gm).astype(BF16)
-        kv = jnp.dot(na, wcat_v[:, 0:256], preferred_element_type=F32)
-        q = jnp.dot(na, wcat_v[:, 256:384], preferred_element_type=F32)
+        return centered * lax.rsqrt(spread + 1e-05)
+
+    def turned(values_in, rows):
         lanes = lax.broadcasted_iota(jnp.int32, (256, 128), 1)
-        cosine = cos_v[rows, :]
-        sine = sin_v[rows, :]
-
-        def turned(values_in):
-            other = jnp.where(lanes < 32, pltpu.roll(values_in, 96, 1), pltpu.roll(values_in, 32, 1))
-            return values_in * cosine + other * sine
-
-        stage_v[0, rows, :] = turned(kv[:, 0:128]).astype(BF16)
-        stage_v[1, rows, :] = kv[:, 128:256].astype(BF16)
-        qstage_v[rows, :] = (turned(q) * (HD**-0.5)).astype(BF16)
-
+        other = jnp.where(lanes < 32, pltpu.roll(values_in, 96, 1), pltpu.roll(values_in, 32, 1))
+        return values_in * cos_v[rows, :] + other * sin_v[rows, :]
+
+    def keys_values(first_step):
+        @pl.loop(first_step, first_step + 2)
+        def _(step):
+            start = lax.rem(step * 256 + (1 - half) * 512, 1024)
+            rows = pl.ds(pl.multiple_of(start, 256), 256)
+            na = (normed_rows(rows) * ga).astype(BF16)
+            na_v[rows, :] = na
+            kv = jnp.dot(na, wcat_v[:, 0:256], preferred_element_type=F32)
+            keys = kv[:, 0:128]
+            keys = jnp.where(jnp.broadcast_to(half, (256, 128)) == 0, turned(keys, rows), keys)
+            stage_v[0, rows, :] = keys.astype(BF16)
+            stage_v[1, rows, :] = kv[:, 128:256].astype(BF16)
+
+    keys_values(0)
     own_keys = pl.ds(pl.multiple_of(half * 512, 512), 512)
     cross_keys = pl.ds(pl.multiple_of((1 - half) * 512, 512), 512)
     kv_cross = remote(stage_v.at[:, cross_keys], kvbuf_v.at[seq, :, :, col_half], partner)
     kv_cross.start()
-    q_cross = remote(qstage_v, q_v.at[:, col_half], partner)
-    q_cross.start()
+    for copy in pair_weights:
+        copy.wait_recv()
+    for copy in seq_weights:
+        copy.start()
+    z_one = []
+    for part in (0, 1):
+        for copies in z_sends[part][1:]:
+            for copy in copies:
+                copy.start()
+        z_one.append(([copy for copies in z_sends[part] for copy in copies], z_own(part)))
+    keys_values(2)
     kv_own = local(stage_v.at[:, own_keys], kvbuf_v.at[seq, :, :, col_half])
-    q_own = local(qstage_v, q_v.at[:, col_half])
-
-    z_one = [z_first(0), z_first(1)]
 
     load_wi.wait()
 
-    @pl.loop(0, 4)
-    def _(step):
-        rows = pl.ds(pl.multiple_of(step * 256, 256), 256)
-        hidden = jnp.dot(nm_v[rows, :], wi_v[...], preferred_element_type=F32)
-        hid_v[rows, :] = (0.5 * hidden * (1.0 + lax.erf(hidden * (0.5**0.5)))).astype(BF16)
+    def mlp_in(first_step):
+        @pl.loop(first_step, first_step + 2)
+        def _(step):
+            rows = pl.ds(pl.multiple_of(step * 256, 256), 256)
+            nm = (normed_rows(rows) * gm).astype(BF16)
+            hidden = jnp.dot(nm, wi_v[...], preferred_element_type=F32)
+            hid_v[rows, :] = (0.5 * hidden * (1.0 + lax.erf(hidden * (0.5**0.5)))).astype(BF16)
+
+    mlp_in(0)
 
     kv_own.wait()
     kv_cross.wait_recv()
@@ -326,6 +353,18 @@
     for k in range(3):
         pl.when(xx == k)(own_out[k][0])
     pl.when(core == 0)(kv_twin(seq).start)
+
+    mlp_in(2)
+
+    for copy in seq_weights[:7]:
+        copy.wait_recv()
+
+    @pl.loop(0, 4)
+    def _(step):
+        rows = pl.ds(pl.multiple_of(step * 256, 256), 256)
+        q = jnp.dot(na_v[rows, :], wcat_v[:, 256:512], preferred_element_type=F32) * (HD**-0.5)
+        q_v[rows, 0:128] = turned(q[:, 0:128], rows).astype(BF16)
+        q_v[rows, 128:256] = q[:, 128:256].astype(BF16)
 
     load_w2.wait()
 
@@ -366,8 +405,6 @@
                 vals_t, weights.astype(BF16), preferred_element_type=F32
             )
 
-    q_own.wait()
-    q_cross.wait_recv()
     attend(seq)
 
     for k in range(4):
@@ -402,11 +439,8 @@
     stat_cross = remote(mine_v, theirs_v, partner)
     stat_cross.start()
     load_wo.wait()
-    wo_cross.wait_recv()
-    wo_twin = remote(wo_v.at[pl.ds(pl.multiple_of((1 - half) * 128 + core * 64, 64), 64), :],
-                     wo_v.at[pl.ds(pl.multiple_of((1 - half) * 128 + core * 64, 64), 64), :], twin)
-    wo_twin.start()
-    wo_twin.wait_recv()
+    for copy in seq_weights[7:]:
+        copy.wait_recv()
     stat_cross.wait_recv()
     top = jnp.maximum(stat_v[0:1, :], theirs_v[0:1, :])
     mine = jnp.exp(stat_v[0:1, :] - top)
@@ -424,8 +458,11 @@
             summed = lax.dot_general(att_v[:, rows], wo_v[:, cols], FF, preferred_element_type=F32)
             part_v[rows, cols] = (part_v[rows, cols].astype(F32) + summed).astype(BF16)
 
+    widths = (640, 384, 512, 512)
+    starts = (0, 640, 1024, 1536)
+
     def cols_of(which):
-        return pl.ds(which * 512, 512)
+        return pl.ds(starts[which], widths[which])
 
     def axis_dev(which, step, first):
         along_y = (which % 2 == 0) == first
@@ -434,6 +471,10 @@
     def scatter(which, first, source, size, direct, relay, sums, merged):
         pos = yy if (which % 2 == 0) == first else zz
         hs = size // 2
+        wide = pl.ds(0, widths[which])
+        direct, relay, sums, merged = (
+            [buf.at[which, k, :, wide] for k in (0, 1)] for buf in (direct, relay, sums, merged)
+        )
 
         def piece(step, part):
             begin = around(pos, step) * size + part * hs
@@ -441,12 +482,12 @@
 
         plus = axis_dev(which, 1, first)
         minus = axis_dev(which, -1, first)
-        r0 = remote(piece(2, 0), relay.at[which, 0], plus)
-        r1 = remote(piece(2, 1), relay.at[which, 1], minus)
-        d0 = remote(piece(1, 1), direct.at[which, 0], plus)
-        d1 = remote(piece(-1, 0), direct.at[which, 1], minus)
-        m0 = remote(sums.at[which, 0], merged.at[which, 0], plus)
-        m1 = remote(sums.at[which, 1], merged.at[which, 1], minus)
+        r0 = remote(piece(2, 0), relay[0], plus)
+        r1 = remote(piece(2, 1), relay[1], minus)
+        d0 = remote(piece(1, 1), direct[0], plus)
+        d1 = remote(piece(-1, 0), direct[1], minus)
+        m0 = remote(sums[0], merged[0], plus)
+        m1 = remote(sums[1], merged[1], minus)
 
         def one():
             for copy in (r0, r1, d0, d1):
@@ -454,10 +495,10 @@
 
         def two():
             r0.wait_recv()
-            sums[which, 0] = (piece(1, 0)[...].astype(F32) + relay[which, 0].astype(F32)).astype(BF16)
+            sums[0][...] = (piece(1, 0)[...].astype(F32) + relay[0][...].astype(F32)).astype(BF16)
             m0.start()
             r1.wait_recv()
-            sums[which, 1] = (piece(-1, 1)[...].astype(F32) + relay[which, 1].astype(F32)).astype(BF16)
+            sums[1][...] = (piece(-1, 1)[...].astype(F32) + relay[1][...].astype(F32)).astype(BF16)
             m1.start()
 
         def three():
@@ -465,8 +506,8 @@
             d1.wait_recv()
             m0.wait_recv()
             m1.wait_recv()
-            lower = piece(0, 0)[...].astype(F32) + direct[which, 1].astype(F32) + merged[which, 0].astype(F32)
-            upper = piece(0, 1)[...].astype(F32) + direct[which, 0].astype(F32) + merged[which, 1].astype(F32)
+            lower = piece(0, 0)[...].astype(F32) + direct[1][...].astype(F32) + merged[0][...].astype(F32)
+            upper = piece(0, 1)[...].astype(F32) + direct[0][...].astype(F32) + merged[1][...].astype(F32)
             return lower, upper
 
         return one, two, three
@@ -477,7 +518,7 @@
         for w in groups
     ]
     second_stage = [
-        scatter(w, False, lambda rows, w=w: fold_v.at[w, rows], 64, direct2_v, relay2_v, sums2_v, merged2_v)
+        scatter(w, False, lambda rows, w=w: fold_v.at[w, rows, pl.ds(0, widths[w])], 64, direct2_v, relay2_v, sums2_v, merged2_v)
         for w in groups
     ]
     for w in groups:
@@ -491,8 +532,8 @@
     x_three.append(along_x(low(0)))
     for w in groups:
         lower, upper = first_stage[w][2]()
-        fold_v[w, 0:128] = lower.astype(BF16)
-        fold_v[w, 128:256] = upper.astype(BF16)
+        fold_v[w, 0:128, 0 : widths[w]] = lower.astype(BF16)
+        fold_v[w, 128:256, 0 : widths[w]] = upper.astype(BF16)
         second_stage[w][0]()
     arrived(y_two[1])
     x_three.append(along_x(high(1)))
@@ -591,7 +632,7 @@
     rot_dims = HD // 4
     powers = np.arange(rot_dims // 2, dtype=np.float32) * np.float32(2.0) / np.float32(rot_dims)
     freqs = np.power(np.float32(10000.0), -powers).astype(np.float32)
-    freqs = jnp.asarray(np.broadcast_to(freqs[:, None], (rot_dims // 2, 128)))
+    freqs = jnp.asarray(np.concatenate([freqs, np.arange(96, dtype=np.float32)])[None, :])
     vmem = pl.BlockSpec(memory_space=pltpu.VMEM)
     hbm = pl.BlockSpec(memory_space=pl.ANY)
     smem = pl.BlockSpec(memory_space=pltpu.SMEM)
@@ -607,8 +648,7 @@
         scratch_shapes=[
             pltpu.VMEM((1024, 2048), BF16),
             pltpu.VMEM((1024, 2048), BF16),
-            pltpu.VMEM((1024, 2048), BF16),
-            pltpu.VMEM((2048, 384), BF16),
+            pltpu.VMEM((2048, 512), BF16),
             pltpu.VMEM((2048, 512), BF16),
             pltpu.VMEM((512, 2048), BF16),
             pltpu.VMEM((256, 2048), BF16),
@@ -621,28 +661,27 @@
             pltpu.VMEM((4, 2, 1024, 256), BF16),
             pltpu.VMEM((8, 2, 512, 256), BF16),
             pltpu.VMEM((2, 1024, 128), BF16),
-            pltpu.VMEM((1024, 128), BF16),
             pltpu.VMEM((1024, 256), BF16),
             pltpu.VMEM((256, 1024), F32),
             pltpu.VMEM((256, 1024), BF16),
             pltpu.VMEM((8, 1024), F32),
             pltpu.VMEM((8, 1024), F32),
             pltpu.VMEM((8, 1024), F32),
-            pltpu.VMEM((4, 2, 128, 512), BF16),
-            pltpu.VMEM((4, 2, 128, 512), BF16),
-            pltpu.VMEM((4, 2, 128, 512), BF16),
-            pltpu.VMEM((4, 2, 128, 512), BF16),
-            pltpu.VMEM((4, 256, 512), BF16),
-            pltpu.VMEM((4, 2, 32, 512), BF16),
-            pltpu.VMEM((4, 2, 32, 512), BF16),
-            pltpu.VMEM((4, 2, 32, 512), BF16),
-            pltpu.VMEM((4, 2, 32, 512), BF16),
+            pltpu.VMEM((4, 2, 128, 640), BF16),
+            pltpu.VMEM((4, 2, 128, 640), BF16),
+            pltpu.VMEM((4, 2, 128, 640), BF16),
+            pltpu.VMEM((4, 2, 128, 640), BF16),
+            pltpu.VMEM((4, 256, 640), BF16),
+            pltpu.VMEM((4, 2, 32, 640), BF16),
+            pltpu.VMEM((4, 2, 32, 640), BF16),
+            pltpu.VMEM((4, 2, 32, 640), BF16),
+            pltpu.VMEM((4, 2, 32, 640), BF16),
             pltpu.VMEM((1024, 128), F32),
             pltpu.VMEM((1024, 128), F32),
             pltpu.VMEM((1, 1024), jnp.int32),
             pltpu.SemaphoreType.DMA((48,)),
-            pltpu.SemaphoreType.DMA((160,)),
-            pltpu.SemaphoreType.DMA((160,)),
+            pltpu.SemaphoreType.DMA((180,)),
+            pltpu.SemaphoreType.DMA((180,)),
             pltpu.SemaphoreType.DMA((16,)),
             pltpu.SemaphoreType.DMA((8, 3)),
         ],

time: 140 us -> 133 us (0.950)
  Pallas kernels: 131 us -> 124 us
    pallas_call x1, Pallas kernels: 131 us -> 124 us  [on_device(): pl.pallas_call(layer_kernel, name='layer', out_shape=(jax.ShapeDtypeStruc...]
where the time goes in v3:
time: 133 us; the launch traced here: 132 us
  Pallas kernels  124 us (93%)
  local copies, waits for them, and re-layouts  6.96 us (5%)
    pallas_call x1, Pallas kernels, on_device(): pl.pallas_call(layer_kernel, name='layer', out_shape=(jax.ShapeDtypeStruc...  124 us
    unnamed x4, local copies, waits for them, and re-layouts  6.96 us

profile of v3, /device:TPU:6, one launch (start us, length us, event | category | flops | bytes accessed | tf_op | source)
XLA Modules:
  0.0 131.9 jit_solution(7263560030036498073)
XLA Ops:
  0.6 124.3 %layer.1 = (bf16[4,256,2048]{2,1,0:T(8,128)(2,1)}, bf16[8,1024,256]{2,1,0:T(8,128)(2,1)}) custom-call(bf16[1024,2048]{1,0:T(8,128)(2,1)} %x_hbm.1, f32[1,2048]{1,0:T(1,128)} %bitcast.10, f32[1,2048]{1,0:T(1,128)} %bitcast.11, bf16[3,2048,128]{2,1,0:T(8,128)(2,1)} %wqkv_hbm.1, bf16[128,2048]{1,0:T(8,128)(2,1)} %wo_hbm.1, bf16[2048,512]{1,0:T(8,128)(2,1)} %wi_hbm.1, ...), custom_call_target="tpu_custom_call" | custom-call | tf_op jit(solution)/shard_map/layer/pallas_call | solution.py:639
  125.0 0.0 copy-start
  125.0 4.9 %copy.16 = bf16[1024,2048]{1,0:T(8,128)(2,1)} copy(bf16[1024,2048]{1,0:T(8,128)(2,1)} %bitcast.8) | data formatting | bytes 8388608
  129.9 0.0 copy-done
  129.9 2.0 %copy.17 = bf16[8,8,2,64,256]{4,3,2,1,0:T(8,128)(2,1)} copy(bf16[8,8,2,64,256]{4,3,2,1,0:T(8,128)(2,1)S(1)} %bitcast.7) | data formatting | bytes 8388608
Async XLA Ops:
  125.0 5.0 %copy-start = (bf16[8,1024,256]{2,1,0:T(8,128)(2,1)S(1)}, bf16[8,1024,256]{2,1,0:T(8,128)(2,1)}, u32[]{:S(2)}) copy-start(bf16[8,1024,256]{2,1,0:T(8,128)(2,1)} %get-tuple-element.5) | copy-start | bytes 12582916

commit v4 on v3

--- a/solution.py
+++ b/solution.py
@@ -29,8 +29,8 @@
     pos_ref,
     psrc_ref,
     kv_hbm,
-    out_hbm,
-    kvout_hbm,
+    out_v,
+    kvout_v,
     x_v,
     na_v,
     wcat_v,
@@ -54,12 +54,9 @@
     theirs_v,
     direct_v,
     relay_v,
-    sums_v,
     merged_v,
-    fold_v,
     direct2_v,
     relay2_v,
-    sums2_v,
     merged2_v,
     cos_v,
     sin_v,
@@ -175,13 +172,13 @@
         return copies, [local(kvs_v.at[pl.ds(yy * 4, 4), low(part)], bufa_v.at[part, yy])]
 
     def then_z(part):
-        copies = [
+        return [
             remote(bufa_v.at[part, :, around(zz, k)], kvx_v.at[:, zh, low(part), col_half], dev(z_=around(zz, k)))
             for k in (1, 3, 2)
         ]
-        for copy in copies:
-            copy.start()
-        return copies, [local(bufa_v.at[part, :, zz], kvx_v.at[:, zh, low(part), col_half])]
+
+    def then_z_own(part):
+        return [local(bufa_v.at[part, :, zz], kvx_v.at[:, zh, low(part), col_half])]
 
     away = 2 * half - 1
 
@@ -215,10 +212,10 @@
         for k in (1, 2, 7, 6, 3, 5, 4):
             to = lax.rem(seq + k, 8)
             copies.append(
-                remote(kvx_v.at[to // 2, lax.rem(to, 2), rows], kvout_hbm.at[seq, rows], (to, ten))
+                remote(kvx_v.at[to // 2, lax.rem(to, 2), rows], kvout_v.at[seq, rows], (to, ten))
             )
             copies[-1].start()
-        return copies, [local(kvx_v.at[xx, core, rows], kvout_hbm.at[seq, rows])]
+        return copies, [local(kvx_v.at[xx, core, rows], kvout_v.at[seq, rows])]
 
     def arrived(stage):
         copies, own = stage
@@ -261,24 +258,32 @@
         other = jnp.where(lanes < 32, pltpu.roll(values_in, 96, 1), pltpu.roll(values_in, 32, 1))
         return values_in * cos_v[rows, :] + other * sin_v[rows, :]
 
-    def keys_values(first_step):
-        @pl.loop(first_step, first_step + 2)
+    def keys_values(first_step, last_step):
+        @pl.loop(first_step, last_step)
         def _(step):
             start = lax.rem(step * 256 + (1 - half) * 512, 1024)
             rows = pl.ds(pl.multiple_of(start, 256), 256)
-            na = (normed_rows(rows) * ga).astype(BF16)
+            normed = normed_rows(rows)
+            na = (normed * ga).astype(BF16)
             na_v[rows, :] = na
+            nm = (normed * gm).astype(BF16)
+            for c in range(16):
+                kvin_v[c, rows, :] = nm[:, c * 128 : (c + 1) * 128]
             kv = jnp.dot(na, wcat_v[:, 0:256], preferred_element_type=F32)
             keys = kv[:, 0:128]
             keys = jnp.where(jnp.broadcast_to(half, (256, 128)) == 0, turned(keys, rows), keys)
             stage_v[0, rows, :] = keys.astype(BF16)
             stage_v[1, rows, :] = kv[:, 128:256].astype(BF16)
 
-    keys_values(0)
     own_keys = pl.ds(pl.multiple_of(half * 512, 512), 512)
-    cross_keys = pl.ds(pl.multiple_of((1 - half) * 512, 512), 512)
-    kv_cross = remote(stage_v.at[:, cross_keys], kvbuf_v.at[seq, :, :, col_half], partner)
-    kv_cross.start()
+    kv_cross = []
+    for step in (0, 1):
+        keys_values(step, step + 1)
+        cross_keys = pl.ds(pl.multiple_of((1 - half) * 512 + step * 256, 256), 256)
+        kv_cross.append(
+            remote(stage_v.at[:, cross_keys], kvbuf_v.at[seq, :, pl.ds(step * 256, 256), col_half], partner)
+        )
+        kv_cross[-1].start()
     for copy in pair_weights:
         copy.wait_recv()
     for copy in seq_weights:
@@ -289,23 +294,22 @@
             for copy in copies:
                 copy.start()
         z_one.append(([copy for copies in z_sends[part] for copy in copies], z_own(part)))
-    keys_values(2)
+    keys_values(2, 4)
     kv_own = local(stage_v.at[:, own_keys], kvbuf_v.at[seq, :, :, col_half])
 
     load_wi.wait()
 
     def mlp_in(first_step):
-        @pl.loop(first_step, first_step + 2)
+        @pl.loop(first_step, first_step + 4)
         def _(step):
             rows = pl.ds(pl.multiple_of(step * 256, 256), 256)
-            nm = (normed_rows(rows) * gm).astype(BF16)
+            nm = jnp.concatenate([kvin_v[c, rows, :] for c in range(16)], axis=1)
             hidden = jnp.dot(nm, wi_v[...], preferred_element_type=F32)
             hid_v[rows, :] = (0.5 * hidden * (1.0 + lax.erf(hidden * (0.5**0.5)))).astype(BF16)
 
-    mlp_in(0)
-
     kv_own.wait()
-    kv_cross.wait_recv()
+    for copy in kv_cross:
+        copy.wait_recv()
 
     def kv_part(slot, part, device, index):
         return pltpu.make_async_remote_copy(
@@ -354,7 +358,7 @@
         pl.when(xx == k)(own_out[k][0])
     pl.when(core == 0)(kv_twin(seq).start)
 
-    mlp_in(2)
+    mlp_in(0)
 
     for copy in seq_weights[:7]:
         copy.wait_recv()
@@ -376,19 +380,21 @@
     z_two = []
     for part in (0, 1):
         arrived(y_one[part])
-        z_two.append(then_z(part))
+        z_two.append((then_z(part), then_z_own(part)))
+    for copy in z_two[0][0]:
+        copy.start()
 
     acc_v[...] = jnp.zeros_like(acc_v)
     stat_v[0:1, :] = jnp.full((1, 1024), LOW, F32)
     stat_v[1:2, :] = jnp.zeros((1, 1024), F32)
 
-    def attend(slot):
+    def attend(slot, first_step=0):
         keys = kvbuf_v[slot, 0]
         vals = kvbuf_v[slot, 1]
         vals_t = vals.T
         key_ids = slot * 1024 + half * 512 + lax.broadcasted_iota(jnp.int32, (512, 1), 0)
 
-        @pl.loop(0, 4)
+        @pl.loop(first_step, 4)
         def _(step):
             cols = pl.ds(pl.multiple_of(step * 256, 256), 256)
             scores = lax.dot_general(keys, q_v[cols, :], TT, preferred_element_type=F32)
@@ -405,7 +411,7 @@
                 vals_t, weights.astype(BF16), preferred_element_type=F32
             )
 
-    attend(seq)
+    attend(seq, 2 * half)
 
     for k in range(4):
 
@@ -458,8 +464,8 @@
             summed = lax.dot_general(att_v[:, rows], wo_v[:, cols], FF, preferred_element_type=F32)
             part_v[rows, cols] = (part_v[rows, cols].astype(F32) + summed).astype(BF16)
 
-    widths = (640, 384, 512, 512)
-    starts = (0, 640, 1024, 1536)
+    widths = (512, 512, 512, 512)
+    starts = (0, 512, 1024, 1536)
 
     def cols_of(which):
         return pl.ds(starts[which], widths[which])
@@ -468,13 +474,11 @@
         along_y = (which % 2 == 0) == first
         return dev(y_=around(yy, step)) if along_y else dev(z_=around(zz, step))
 
-    def scatter(which, first, source, size, direct, relay, sums, merged):
+    def scatter(which, first, source, size, direct, relay, merged):
         pos = yy if (which % 2 == 0) == first else zz
         hs = size // 2
         wide = pl.ds(0, widths[which])
-        direct, relay, sums, merged = (
-            [buf.at[which, k, :, wide] for k in (0, 1)] for buf in (direct, relay, sums, merged)
-        )
+        direct, relay, merged = ([buf.at[which, k, :, wide] for k in (0, 1)] for buf in (direct, relay, merged))
 
         def piece(step, part):
             begin = around(pos, step) * size + part * hs
@@ -486,8 +490,8 @@
         r1 = remote(piece(2, 1), relay[1], minus)
         d0 = remote(piece(1, 1), direct[0], plus)
         d1 = remote(piece(-1, 0), direct[1], minus)
-        m0 = remote(sums[0], merged[0], plus)
-        m1 = remote(sums[1], merged[1], minus)
+        m0 = remote(relay[0], merged[0], plus)
+        m1 = remote(relay[1], merged[1], minus)
 
         def one():
             for copy in (r0, r1, d0, d1):
@@ -495,10 +499,10 @@
 
         def two():
             r0.wait_recv()
-            sums[0][...] = (piece(1, 0)[...].astype(F32) + relay[0][...].astype(F32)).astype(BF16)
+            relay[0][...] = (piece(1, 0)[...].astype(F32) + relay[0][...].astype(F32)).astype(BF16)
             m0.start()
             r1.wait_recv()
-            sums[1][...] = (piece(-1, 1)[...].astype(F32) + relay[1][...].astype(F32)).astype(BF16)
+            relay[1][...] = (piece(-1, 1)[...].astype(F32) + relay[1][...].astype(F32)).astype(BF16)
             m1.start()
 
         def three():
@@ -513,12 +517,20 @@
         return one, two, three
 
     groups = range(4)
+    base_of = (yy * 256, zz * 256) * 2
+
+    def own_chunk(w, begin, size):
+        return part_v.at[pl.ds(pl.multiple_of(base_of[w] + begin, 32), size), cols_of(w)]
+
+    def fold(w, begin, value):
+        part_v[pl.ds(pl.multiple_of(base_of[w] + begin, 128), 128), cols_of(w)] = value.astype(BF16)
+
     first_stage = [
-        scatter(w, True, lambda rows, w=w: part_v.at[rows, cols_of(w)], 256, direct_v, relay_v, sums_v, merged_v)
+        scatter(w, True, lambda rows, w=w: part_v.at[rows, cols_of(w)], 256, direct_v, relay_v, merged_v)
         for w in groups
     ]
     second_stage = [
-        scatter(w, False, lambda rows, w=w: fold_v.at[w, rows, pl.ds(0, widths[w])], 64, direct2_v, relay2_v, sums2_v, merged2_v)
+        scatter(w, False, lambda rows, w=w: own_chunk(w, rows.start, rows.size), 64, direct2_v, relay2_v, merged2_v)
         for w in groups
     ]
     for w in groups:
@@ -528,21 +540,21 @@
     x_three = [along_x(high(0))]
     for w in groups:
         first_stage[w][1]()
+    for copy in z_two[1][0][:2]:
+        copy.start()
     arrived(z_two[0])
     x_three.append(along_x(low(0)))
     for w in groups:
         lower, upper = first_stage[w][2]()
-        fold_v[w, 0:128, 0 : widths[w]] = lower.astype(BF16)
-        fold_v[w, 128:256, 0 : widths[w]] = upper.astype(BF16)
+        fold(w, 0, lower)
+        fold(w, 128, upper)
         second_stage[w][0]()
+    z_two[1][0][2].start()
     arrived(y_two[1])
     x_three.append(along_x(high(1)))
-    arrived(z_two[1])
-    x_three.append(along_x(low(1)))
     for w in groups:
         second_stage[w][1]()
 
-    base_of = (yy * 256, zz * 256) * 2
     small_of = (zz, yy) * 2
 
     def gather(which, first, base, size):
@@ -552,8 +564,8 @@
         def rows_at(step, part=None):
             begin = base + around(pos, step) * size
             if part is None:
-                return na_v.at[pl.ds(pl.multiple_of(begin, size), size), cols_of(which)]
-            return na_v.at[pl.ds(pl.multiple_of(begin + part * hs, hs), hs), cols_of(which)]
+                return out_v.at[pl.ds(pl.multiple_of(begin, size), size), cols_of(which)]
+            return out_v.at[pl.ds(pl.multiple_of(begin + part * hs, hs), hs), cols_of(which)]
 
         plus = axis_dev(which, 1, first)
         minus = axis_dev(which, -1, first)
@@ -586,8 +598,10 @@
         begin = base_of[w] + small_of[w] * 64
         for part, value in ((0, lower), (1, upper)):
             rows = pl.ds(pl.multiple_of(begin + part * 32, 32), 32)
-            na_v[rows, cols_of(w)] = (x_v[rows, cols_of(w)].astype(F32) + value).astype(BF16)
+            out_v[rows, cols_of(w)] = (x_v[rows, cols_of(w)].astype(F32) + value).astype(BF16)
         small_gather[w][0]()
+    arrived(z_two[1])
+    x_three.append(along_x(low(1)))
     for w in groups:
         small_gather[w][1]()
     for w in groups:
@@ -597,11 +611,8 @@
         large_gather[w][1]()
     for w in groups:
         large_gather[w][2]()
-    out_copies = [local(na_v.at[pl.ds(k * 256, 256)], out_hbm.at[k]) for k in range(4)]
     for stage in x_three:
         arrived(stage)
-    for copy in out_copies:
-        copy.wait()
     for copy in pending:
         copy.wait_send()
     for k in range(3):
@@ -640,11 +651,11 @@
         layer_kernel,
         name="layer",
         out_shape=(
-            jax.ShapeDtypeStruct((4, 256, 2048), BF16),
-            jax.ShapeDtypeStruct((8, 1024, 256), BF16),
+            pltpu.VMEM((1024, 2048), BF16),
+            pltpu.VMEM((8, 1024, 256), BF16),
         ),
         in_specs=[hbm, vmem, vmem, hbm, hbm, hbm, hbm, vmem, vmem, vmem, smem, hbm],
-        out_specs=(hbm, hbm),
+        out_specs=(vmem, vmem),
         scratch_shapes=[
             pltpu.VMEM((1024, 2048), BF16),
             pltpu.VMEM((1024, 2048), BF16),
@@ -667,15 +678,12 @@
             pltpu.VMEM((8, 1024), F32),
             pltpu.VMEM((8, 1024), F32),
             pltpu.VMEM((8, 1024), F32),
-            pltpu.VMEM((4, 2, 128, 640), BF16),
-            pltpu.VMEM((4, 2, 128, 640), BF16),
-            pltpu.VMEM((4, 2, 128, 640), BF16),
-            pltpu.VMEM((4, 2, 128, 640), BF16),
-            pltpu.VMEM((4, 256, 640), BF16),
-            pltpu.VMEM((4, 2, 32, 640), BF16),
-            pltpu.VMEM((4, 2, 32, 640), BF16),
-            pltpu.VMEM((4, 2, 32, 640), BF16),
-            pltpu.VMEM((4, 2, 32, 640), BF16),
+            pltpu.VMEM((4, 2, 128, 512), BF16),
+            pltpu.VMEM((4, 2, 128, 512), BF16),
+            pltpu.VMEM((4, 2, 128, 512), BF16),
+            pltpu.VMEM((4, 2, 32, 512), BF16),
+            pltpu.VMEM((4, 2, 32, 512), BF16),
+            pltpu.VMEM((4, 2, 32, 512), BF16),
             pltpu.VMEM((1024, 128), F32),
             pltpu.VMEM((1024, 128), F32),
             pltpu.VMEM((1, 1024), jnp.int32),
@@ -686,7 +694,7 @@
             pltpu.SemaphoreType.DMA((8, 3)),
         ],
         compiler_params=pltpu.CompilerParams(
-            collective_id=0, has_side_effects=True, vmem_limit_bytes=67043328
+            collective_id=0, has_side_effects=True, vmem_limit_bytes=58600000
         ),
     )(
         hidden_in,
@@ -702,7 +710,7 @@
         page_source,
         kv_prefill.reshape(16, 1024, 128),
     )
-    return (out.reshape(1024, 2048), pages.reshape(8, 8, 2, 64, 256))
+    return (out, pages.reshape(8, 8, 2, 64, 256))
 
 
 def solution(mesh):

time: 133 us -> 131 us (0.985)
  local copies, waits for them, and re-layouts: 6.96 us -> 4.03 us
  Pallas kernels: 124 us -> 126 us
    unnamed x4 -> x2, local copies, waits for them, and re-layouts: 6.96 us -> 4.03 us
    pallas_call x1, Pallas kernels: 124 us -> 126 us  [on_device(): pl.pallas_call(layer_kernel, name='layer', out_shape=(pltpu.VMEM((1024, 2...]
where the time goes in v4:
time: 131 us
  Pallas kernels  126 us (96%)
  local copies, waits for them, and re-layouts  4.03 us (3%)
    pallas_call x1, Pallas kernels, on_device(): pl.pallas_call(layer_kernel, name='layer', out_shape=(pltpu.VMEM((1024, 2...  126 us
    unnamed x2, local copies, waits for them, and re-layouts  4.03 us

profile of v4, /device:TPU:6, one launch (start us, length us, event | category | flops | bytes accessed | tf_op | source)
XLA Modules:
  0.0 130.6 jit_solution(17746657203341197675)
XLA Ops:
  0.6 125.9 %layer.1 = (bf16[1024,2048]{1,0:T(8,128)(2,1)S(1)}, bf16[8,1024,256]{2,1,0:T(8,128)(2,1)S(1)}) custom-call(bf16[1024,2048]{1,0:T(8,128)(2,1)} %x_hbm.1, f32[1,2048]{1,0:T(1,128)} %bitcast.8, f32[1,2048]{1,0:T(1,128)} %bitcast.9, bf16[3,2048,128]{2,1,0:T(8,128)(2,1)} %wqkv_hbm.1, bf16[128,2048]{1,0:T(8,128)(2,1)} %wo_hbm.1, bf16[2048,512]{1,0:T(8,128)(2,1)} %wi_hbm.1, ...), custom_call_target="tpu_custom_call" | custom-call | tf_op jit(solution)/shard_map/layer/pallas_call | solution.py:650
  126.6 2.0 %copy.16 = bf16[1024,2048]{1,0:T(8,128)(2,1)} copy(bf16[1024,2048]{1,0:T(8,128)(2,1)S(1)} %get-tuple-element.6) | data formatting | bytes 8388608
  128.6 2.0 %copy.17 = bf16[8,8,2,64,256]{4,3,2,1,0:T(8,128)(2,1)} copy(bf16[8,8,2,64,256]{4,3,2,1,0:T(8,128)(2,1)S(1)} %bitcast.6) | data formatting | bytes 8388608
